TPU v7x, 512 devices: a whole 4x4x16 slice. The times are simulated.
512 devices in a mesh: dp: 16 (over z), segment: 2 (over y_hi), tensor: 16 (over x, y_lo, core).
Axes of the slice: x: 4, y: 4 (y_hi: 2, y_lo: 2; y = y_hi * 2 + y_lo), z: 16, core: 2. Of those that a mesh axis runs over, the one named last changes fastest.
Arguments:
- context: bfloat16 [1152, 4096], P(None, 'tensor'), may hold values from -6 to 6
- residual: bfloat16 [1152, 4096], P(None, 'dp'), may hold values from -6 to 6
- inverse_rms: float32 [1152], replicated, may hold values from 0.5 to 2
- norm_gain: float32 [4096], P('dp'), may hold values from 0.5 to 1.5
- gate_preact: bfloat16 [1152, 14336], P(None, 'tensor'), may hold values from -6 to 6
- up_preact: bfloat16 [1152, 14336], P(None, 'tensor'), may hold values from -6 to 6
- upstream: bfloat16 [1152, 4096], P(None, 'dp'), may hold values from -6 to 6
- gate_weight: bfloat16 [4096, 14336], P('dp', 'tensor'), may hold values from -0.09375 to 0.09375
- up_weight: bfloat16 [4096, 14336], P('dp', 'tensor'), may hold values from -0.09375 to 0.09375
- down_weight: bfloat16 [14336, 4096], P('tensor', 'dp'), may hold values from -0.046875 to 0.046875
- policy_logprob: float32 [32], replicated, may hold values from -270 to -230
- ref_logprob: float32 [32], replicated, may hold values from -270 to -230
- lengths: int32 [32], replicated, may hold values from 4061 to 4096
Outputs:
- residual_grad: bfloat16 [1152, 4096], P('tensor', 'dp')
- output_weight_grad: bfloat16 [4096, 4096], P('tensor', ('dp', 'segment'))
- gate_weight_grad: bfloat16 [4096, 14336], P(('dp', 'segment'), 'tensor')
- up_weight_grad: bfloat16 [4096, 14336], P(('dp', 'segment'), 'tensor')
- down_weight_grad: bfloat16 [14336, 4096], P('tensor', ('dp', 'segment'))
Inputs may be any that keep to these rules, and one draw needn't show every extreme that they name: `lengths`: the window holds positions 4060 to 4095 of every sequence; a position counts where it is below the sequence's length.
All inputs are finite; a program needn't handle non-finite values.
Results may differ from a plain program's by a relative error of at most 0.03.
Values may be sent and summed in bfloat16 or wider, within the bound.
A program may use at most 64 MiB of HBM per device.

v0:
```python
import jax
import jax.numpy as jnp
from jax import lax
from jax.sharding import PartitionSpec as P

D = 4096
POS = 36
LEN = 4096


def shifted(value, axis, steps):
    count = lax.axis_size(axis)
    first, last = (max(0, -steps), min(count, count - steps))
    return lax.ppermute(value, axis, [(source, source + steps) for source in range(first, last)])


def from_partner(value, axis, apart):
    mask = 2**apart
    pairs = [(source, source ^ mask) for source in range(lax.axis_size(axis))]
    return lax.ppermute(value, axis, pairs)


def token_weights(policy_logprob, ref_logprob, lengths, total_rows):
    npo_weight = 2.0 * jax.nn.sigmoid(0.1 * (policy_logprob - ref_logprob))
    positions = jnp.arange(total_rows, dtype=jnp.int32)
    sequence_of = positions // POS
    position_in = LEN - POS + positions % POS
    member = sequence_of[:, None] == jnp.arange(policy_logprob.shape[0], dtype=jnp.int32)[None, :]
    weight = jnp.sum(jnp.where(member, npo_weight[None, :], 0.0), axis=1)
    length_of = jnp.sum(jnp.where(member, lengths[None, :], 0), axis=1)
    return jnp.where(position_in < length_of, weight, 0.0)


def gate_grads_of(hidden_delta, gate_value, up_value):
    squash = jax.nn.sigmoid(gate_value)
    gate_delta = (hidden_delta * up_value * squash * (1.0 + gate_value * (1.0 - squash))).astype(
        jnp.bfloat16
    )
    up_delta = (hidden_delta * gate_value * squash).astype(jnp.bfloat16)
    return (gate_delta, up_delta)


def row_statistic(partial_dot):
    return lax.psum(partial_dot, "dp")


def finish_rows(weighted, residual, inverse_rms, norm_gain, normed_delta):
    residual_value = residual.astype(jnp.float32)
    row_dot = row_statistic(jnp.sum(norm_gain[None, :] * normed_delta * residual_value, axis=1))
    row_scale = inverse_rms * inverse_rms * inverse_rms * row_dot / D
    combined = (
        weighted.astype(jnp.float32)
        + inverse_rms[:, None] * norm_gain[None, :] * normed_delta
        - residual_value * row_scale[:, None]
    )
    return combined.astype(jnp.bfloat16)


def shards(
    context,
    residual,
    inverse_rms,
    norm_gain,
    gate_preact,
    up_preact,
    upstream,
    gate_weight,
    up_weight,
    down_weight,
    policy_logprob,
    ref_logprob,
    lengths,
):
    ffn_side = lax.axis_index("segment") == 1
    total_rows = residual.shape[0]
    features = residual.shape[1]
    hidden_width = gate_preact.shape[1]
    half_width = features // 2
    share_rows = total_rows // lax.axis_size("tensor")
    share_start = lax.axis_index("tensor") * share_rows
    token_weight = token_weights(policy_logprob, ref_logprob, lengths, total_rows)
    weighted = (upstream.astype(jnp.float32) * token_weight[:, None]).astype(jnp.bfloat16)
    normed = (residual.astype(jnp.float32) * inverse_rms[:, None] * norm_gain[None, :]).astype(
        jnp.bfloat16
    )
    gate_value = gate_preact.astype(jnp.float32)
    up_value = up_preact.astype(jnp.float32)
    hidden = (gate_value * jax.nn.sigmoid(gate_value) * up_value).astype(jnp.bfloat16)

    def down_part():
        return jnp.einsum("tf,td->fd", hidden, weighted, preferred_element_type=jnp.float32)

    down_full = lax.cond(
        ffn_side, down_part, lambda: jnp.zeros((hidden_width, features), jnp.float32)
    )
    hidden_delta = lax.psum(
        lax.cond(
            ffn_side,
            lambda: jnp.einsum(
                "td,fd->tf", weighted, down_weight, preferred_element_type=jnp.float32
            ),
            lambda: jnp.zeros((total_rows, hidden_width), jnp.float32),
        ).astype(jnp.bfloat16),
        "dp",
    ).astype(jnp.float32)
    gate_delta, up_delta = gate_grads_of(hidden_delta, gate_value, up_value)

    def weight_parts():
        gate_full = jnp.einsum("td,tf->df", normed, gate_delta, preferred_element_type=jnp.float32)
        up_full = jnp.einsum("td,tf->df", normed, up_delta, preferred_element_type=jnp.float32)
        return (gate_full, up_full)

    empty_grad = jnp.zeros((features, hidden_width), jnp.float32)
    gate_full, up_full = lax.cond(ffn_side, weight_parts, lambda: (empty_grad, empty_grad))

    def product():
        first_term = jnp.einsum(
            "tf,df->td", gate_delta, gate_weight, preferred_element_type=jnp.float32
        )
        return first_term + jnp.einsum(
            "tf,df->td", up_delta, up_weight, preferred_element_type=jnp.float32
        )

    normed_delta = lax.psum(
        lax.cond(ffn_side, product, lambda: jnp.zeros((total_rows, features), jnp.float32)).astype(
            jnp.bfloat16
        ),
        "tensor",
    ).astype(jnp.float32)
    grad_every = finish_rows(weighted, residual, inverse_rms, norm_gain, normed_delta)
    arrived = shifted(grad_every, "segment", -1)
    grad_tokens = jnp.where(ffn_side, grad_every, arrived)
    residual_grad = lax.dynamic_slice_in_dim(grad_tokens, share_start, share_rows, 0)

    def projection_part():
        return jnp.einsum("tc,td->cd", context, grad_tokens, preferred_element_type=jnp.float32)

    projection_full = lax.cond(
        ffn_side, lambda: jnp.zeros((context.shape[1], features), jnp.float32), projection_part
    )
    projection_bf = projection_full.astype(jnp.bfloat16)
    gate_bf = gate_full.astype(jnp.bfloat16)
    up_bf = up_full.astype(jnp.bfloat16)
    down_bf = down_full.astype(jnp.bfloat16)
    got_projection, got_gate, got_up, got_down = from_partner(
        (
            projection_bf[:, half_width:],
            gate_bf[:half_width],
            up_bf[:half_width],
            down_bf[:, :half_width],
        ),
        "segment",
        0,
    )
    output_weight_grad = jnp.where(ffn_side, got_projection, projection_bf[:, :half_width])
    gate_weight_grad = jnp.where(ffn_side, gate_bf[half_width:], got_gate)
    up_weight_grad = jnp.where(ffn_side, up_bf[half_width:], got_up)
    down_weight_grad = jnp.where(ffn_side, down_bf[:, half_width:], got_down)
    return (residual_grad, output_weight_grad, gate_weight_grad, up_weight_grad, down_weight_grad)


def solution(mesh):
    return jax.shard_map(
        shards,
        mesh=mesh,
        in_specs=(
            P(None, "tensor"),
            P(None, "dp"),
            P(),
            P("dp"),
            P(None, "tensor"),
            P(None, "tensor"),
            P(None, "dp"),
            P("dp", "tensor"),
            P("dp", "tensor"),
            P("tensor", "dp"),
            P(),
            P(),
            P(),
        ),
        out_specs=(
            P("tensor", "dp"),
            P("tensor", ("dp", "segment")),
            P(("dp", "segment"), "tensor"),
            P(("dp", "segment"), "tensor"),
            P("tensor", ("dp", "segment")),
        ),
        check_vma=False,
    )
```

profile of v0, /device:TPU:6, one launch (start us, length us, event | category | flops | bytes accessed | tf_op | source)
XLA Modules:
  0.0 374.8 jit_solution(5367766257168562192)
XLA Ops:
  7.2 0.0 all-reduce.3.cloned.1.call-start
  7.2 0.7 divide_multiply_fusion
  7.9 0.1 select_reduce_fusion
  8.0 0.8 select_reduce_fusion.1
  8.8 1.3 multiply_convert_fusion
  10.1 0.2 conditional.5
  10.1 0.2 broadcast.64
  10.3 0.0 copy-start.2
  10.3 1.3 copy-done.2
  11.6 0.0 all-reduce.3.cloned.1.call-update
  11.6 0.0 all-reduce.5.cloned.1.call-start
  11.7 150.1 %all-reduce.3.cloned.1.call-done = bf16[1152,896]{1,0:T(8,128)(2,1)} async-done(((bf16[1152,896]{1,0:T(8,128)(2,1)}), bf16[1152,896]{1,0:T(8,128)(2,1)}) %all-reduce.3.cloned.1.call-update) | async-done | bytes 2064400 | tf_op jit(solution)/shard_map/psum | solution.py:96
  161.8 5.8 %fusion.3 = (bf16[1152,896]{1,0:T(8,128)(2,1)}, bf16[1152,896]{1,0:T(8,128)(2,1)S(1)}, bf16[1152,896]{1,0:T(8,128)(2,1)}) fusion(bf16[1152,896]{1,0:T(8,128)(2,1)} %param.28, bf16[1152,896]{1,0:T(8,128)(2,1)} %param.27, bf16[1152,896]{1,0:T(8,128)(2,1)} %all-reduce.3.cloned.1.call-done), kind=kLoop, calls=%fused_computation.10 | loop fusion | flops 19611648 | bytes 12386304 | tf_op jit(solution)/shard_map/convert_element_type | solution.py:88
  167.6 0.0 copy-start.3
  167.6 0.8 copy-done.3
  168.4 0.0 all-reduce.5.cloned.1.call-update
  168.5 0.0 copy-start.5
  168.5 0.0 copy-start.9
  168.5 0.0 copy-start.8
  168.5 0.8 conditional.9
  168.5 0.8 broadcast.67
  169.3 0.0 copy-start.4
  169.3 1.0 slice.39
  170.4 10.1 %collective-permute-start.4 = (bf16[896,128]{1,0:T(8,128)(2,1)S(1)}, bf16[896,128]{1,0:T(8,128)(2,1)}, u32[]{:S(2)}, u32[]{:S(2)}) collective-permute-start(bf16[896,128]{1,0:T(8,128)(2,1)S(1)} %slice.39), channel_id=1, source_target_pairs={{0,16},{16,0},{1,17},{17,1},{2,18},{18,2},{3,19},{19,3},{4,20},{20... | collective-permute-start | bytes 688136 | tf_op jit(solution)/shard_map/ppermute | solution.py:20
  180.5 114.9 %all-reduce.5.cloned.1.call-done = bf16[1152,256]{1,0:T(8,128)(2,1)} async-done(((bf16[1152,256]{1,0:T(8,128)(2,1)}), bf16[1152,256]{1,0:T(8,128)(2,1)}) %all-reduce.5.cloned.1.call-update) | async-done | bytes 589840 | tf_op jit(solution)/shard_map/psum | solution.py:124
  295.3 0.0 copy-done.5
  295.3 0.0 copy-done.9
  295.4 1.3 fusion.13
  296.7 30.8 %psum.23 = f32[1152]{0:T(1024)S(1)} all-reduce(f32[1152]{0:T(1024)S(1)} %fusion.13), channel_id=1, replica_groups=mesh['dp'=16,'segment'=2,'tensor'=16] {'dp'}, use_global_device_ids=true, to_apply=%region_9.10 | all-reduce | flops 1152 | bytes 9216 | tf_op jit(solution)/shard_map/psum | solution.py:44
  327.5 0.0 copy-done.8
  327.5 0.0 copy-start
  327.5 0.0 copy-done.4
  327.5 2.7 fusion.15
  330.2 0.0 copy-done
  330.2 0.0 copy-start.6
  330.2 0.1 conditional.8
  330.4 6.5 %collective-permute-start.3 = (bf16[128,896]{1,0:T(8,128)(2,1)S(1)}, bf16[128,896]{1,0:T(8,128)(2,1)S(1)}, u32[]{:S(2)}, u32[]{:S(2)}) collective-permute-start(bf16[128,896]{1,0:T(8,128)(2,1)S(1)} %slice.37), channel_id=1, source_target_pairs={{0,16},{16,0},{1,17},{17,1},{2,18},{18,2},{3,19},{19,3},{4,20},{20... | collective-permute-start | bytes 688136 | tf_op jit(solution)/shard_map/ppermute | solution.py:20
  336.9 0.0 copy-done.6
  336.9 0.0 copy-start.10
  336.9 1.4 collective-permute-start
  338.4 0.0 collective-permute-done.4
  338.4 1.8 slice_select_fusion
  340.2 6.0 %collective-permute-start.2 = (bf16[128,896]{1,0:T(8,128)(2,1)S(1)}, bf16[128,896]{1,0:T(8,128)(2,1)S(1)}, u32[]{:S(2)}, u32[]{:S(2)}) collective-permute-start(bf16[128,896]{1,0:T(8,128)(2,1)S(1)} %slice.35), channel_id=1, source_target_pairs={{0,16},{16,0},{1,17},{17,1},{2,18},{18,2},{3,19},{19,3},{4,20},{20... | collective-permute-start | bytes 688136 | tf_op jit(solution)/shard_map/ppermute | solution.py:20
  346.2 0.0 collective-permute-done.3
  346.2 0.7 slice_select_fusion.1
  346.9 11.6 %collective-permute-done.2 = bf16[128,896]{1,0:T(8,128)(2,1)S(1)} collective-permute-done((bf16[128,896]{1,0:T(8,128)(2,1)S(1)}, bf16[128,896]{1,0:T(8,128)(2,1)S(1)}, u32[]{:S(2)}, u32[]{:S(2)}) %collective-permute-start.2) | collective-permute-done | bytes 229408 | tf_op jit(solution)/shard_map/ppermute | solution.py:20
  358.5 0.7 slice_select_fusion.2
  359.2 0.0 collective-permute-done
  359.2 0.1 broadcast_select_fusion
  359.2 0.0 copy-done.10
  359.3 0.4 conditional.7
  359.3 0.4 fusion.27
  359.7 1.9 collective-permute-start.1
  361.6 0.6 constant_dynamic-slice_fusion
  362.2 5.1 %collective-permute-done.1 = bf16[256,128]{1,0:T(8,128)(2,1)S(1)} collective-permute-done((bf16[256,128]{1,0:T(8,128)(2,1)S(1)}, bf16[256,128]{1,0:T(8,128)(2,1)S(1)}, u32[]{:S(2)}, u32[]{:S(2)}) %collective-permute-start.1) | collective-permute-done | bytes 65568 | tf_op jit(solution)/shard_map/ppermute | solution.py:20
  367.3 0.6 slice_select_fusion.3
  (10 shorter events, 0.2 us)
Async XLA Ops:
  7.2 154.7 %all-reduce.3.cloned.1.call-start = ((), (), s32[]{:S(2)}) async-start(), calls=%async_computation | async-start | bytes 4128768 | tf_op jit(solution)/shard_map/psum | solution.py:96
  10.3 1.3 copy-start.2
  11.6 283.7 %all-reduce.5.cloned.1.call-start = ((), (), s32[]{:S(2)}) async-start(), calls=%async_computation.1 | async-start | bytes 1179648 | tf_op jit(solution)/shard_map/psum | solution.py:124
  167.6 0.8 copy-start.3
  168.5 126.9 %copy-start.5 = (bf16[1152,256]{1,0:T(8,128)(2,1)S(1)}, bf16[1152,256]{1,0:T(8,128)(2,1)}, u32[]{:S(2)}) copy-start(bf16[1152,256]{1,0:T(8,128)(2,1)} %param.24) | copy-start | bytes 1769476
  168.5 126.9 %copy-start.9 = (f32[256]{0:T(256)S(1)}, f32[256]{0:T(256)}, u32[]{:S(2)}) copy-start(f32[256]{0:T(256)} %param.26) | copy-start | bytes 3076
  168.5 159.0 %copy-start.8 = (f32[1152]{0:T(1024)S(1)}, f32[1152]{0:T(1024)}, u32[]{:S(2)}) copy-start(f32[1152]{0:T(1024)} %param.25) | copy-start | bytes 13828
  169.3 158.2 %copy-start.4 = (bf16[1152,256]{1,0:T(8,128)(2,1)S(1)}, bf16[1152,256]{1,0:T(8,128)(2,1)}, u32[]{:S(2)}) copy-start(bf16[1152,256]{1,0:T(8,128)(2,1)} %param.29) | copy-start | bytes 1769476
  170.4 168.0 %collective-permute-start.4 = (bf16[896,128]{1,0:T(8,128)(2,1)S(1)}, bf16[896,128]{1,0:T(8,128)(2,1)}, u32[]{:S(2)}, u32[]{:S(2)}) collective-permute-start(bf16[896,128]{1,0:T(8,128)(2,1)S(1)} %slice.39), channel_id=1, source_target_pairs={{0,16},{16,0},{1,17},{17,1},{2,18},{18,2},{3,19},{19,3},{4,20},{20... | collective-permute-start | bytes 688136 | tf_op jit(solution)/shard_map/ppermute | solution.py:20
  327.5 2.7 copy-start
  330.2 6.7 %copy-start.6 = (bf16[1152,256]{1,0:T(8,128)(2,1)S(1)}, bf16[1152,256]{1,0:T(8,128)(2,1)}, u32[]{:S(2)}) copy-start(bf16[1152,256]{1,0:T(8,128)(2,1)} %get-tuple-element.72) | copy-start | bytes 1769476
  330.4 15.8 %collective-permute-start.3 = (bf16[128,896]{1,0:T(8,128)(2,1)S(1)}, bf16[128,896]{1,0:T(8,128)(2,1)S(1)}, u32[]{:S(2)}, u32[]{:S(2)}) collective-permute-start(bf16[128,896]{1,0:T(8,128)(2,1)S(1)} %slice.37), channel_id=1, source_target_pairs={{0,16},{16,0},{1,17},{17,1},{2,18},{18,2},{3,19},{19,3},{4,20},{20... | collective-permute-start | bytes 688136 | tf_op jit(solution)/shard_map/ppermute | solution.py:20
  336.9 22.3 %copy-start.10 = (bf16[1152,256]{1,0:T(8,128)(2,1)S(1)}, bf16[1152,256]{1,0:T(8,128)(2,1)}, u32[]{:S(2)}) copy-start(bf16[1152,256]{1,0:T(8,128)(2,1)} %param.23) | copy-start | bytes 1769476
  336.9 22.2 %collective-permute-start = (bf16[1152,256]{1,0:T(8,128)(2,1)S(1)}, bf16[1152,256]{1,0:T(8,128)(2,1)S(1)}, u32[]{:S(2)}, u32[]{:S(2)}) collective-permute-start(bf16[1152,256]{1,0:T(8,128)(2,1)S(1)} %copy-done.6), channel_id=1, source_target_pairs={{16,0},{17,1},{18,2},{19,3},{20,4},{21,5},{22,6},{23,7},{24,8},{25... | collective-permute-start | bytes 1769480 | tf_op jit(solution)/shard_map/ppermute | solution.py:14
  340.2 18.3 %collective-permute-start.2 = (bf16[128,896]{1,0:T(8,128)(2,1)S(1)}, bf16[128,896]{1,0:T(8,128)(2,1)S(1)}, u32[]{:S(2)}, u32[]{:S(2)}) collective-permute-start(bf16[128,896]{1,0:T(8,128)(2,1)S(1)} %slice.35), channel_id=1, source_target_pairs={{0,16},{16,0},{1,17},{17,1},{2,18},{18,2},{3,19},{19,3},{4,20},{20... | collective-permute-start | bytes 688136 | tf_op jit(solution)/shard_map/ppermute | solution.py:20
  359.7 7.7 %collective-permute-start.1 = (bf16[256,128]{1,0:T(8,128)(2,1)S(1)}, bf16[256,128]{1,0:T(8,128)(2,1)S(1)}, u32[]{:S(2)}, u32[]{:S(2)}) collective-permute-start(bf16[256,128]{1,0:T(8,128)(2,1)S(1)} %slice.32), channel_id=1, source_target_pairs={{0,16},{16,0},{1,17},{17,1},{2,18},{18,2},{3,19},{19,3},{4,20},{20... | collective-permute-start | bytes 196616 | tf_op jit(solution)/shard_map/ppermute | solution.py:20
Sparse Core Ops, SparseCore 0:
  11.7 150.0 all-reduce.2
  168.6 126.7 all-reduce.4
where the time goes:
time: 376 us; the launch traced here: 375 us
  waiting for transfers between devices  282 us (75%)
  blocking collectives  30.8 us (8%)
  starting transfers between devices  26.1 us (7%)
  other arithmetic  16.6 us (4%)
  between operations  14.3 us (4%)
  local copies, waits for them, and re-layouts  4.94 us (1%)
    psum x1, waiting for transfers between devices, shards(): lax.psum(lax.cond(ffn_side, lambda: jnp.einsum('td,fd->tf', weighted, dow...  150 us
    psum x1, waiting for transfers between devices, shards(): lax.psum(lax.cond(ffn_side, product, lambda: jnp.zeros((total_rows, featu...  115 us
    psum x1, blocking collectives, row_statistic(): return lax.psum(partial_dot, 'dp')  30.8 us
    ppermute x4, starting transfers between devices, from_partner(): return lax.ppermute(value, axis, pairs)  24.6 us
    ppermute x4, waiting for transfers between devices, from_partner(): return lax.ppermute(value, axis, pairs)  16.7 us
  transfers between devices with their start and end apart: 7, of which 4 were waited for; matrix products, arithmetic and copies ran while one was open for 3% of the time, Pallas kernels for 0%

commit v1 on v0

v1 whole, which is shorter than its diff:
```python
import functools
import math

import jax
import jax.numpy as jnp
from jax import lax
from jax.experimental import pallas as pl
from jax.experimental.pallas import tpu as pltpu
from jax.sharding import PartitionSpec as P

POS = 36
LEN = 4096
PIECES = 4
MESH = pl.DeviceIdType.MESH
BF16 = jnp.bfloat16
F32 = jnp.float32


def wrapped(value, count):
    return lax.rem(value + count, count)


def dot_nt(a, b):
    return lax.dot_general(a, b, (((1,), (1,)), ((), ())), preferred_element_type=F32)


def dot_tn(a, b):
    return lax.dot_general(a, b, (((0,), (0,)), ((), ())), preferred_element_type=F32)


def kernel(
    size,
    context_hbm,
    residual_hbm,
    rms_row,
    gain_row,
    gate_hbm,
    up_hbm,
    upstream_hbm,
    gate_weight_hbm,
    up_weight_hbm,
    down_weight_hbm,
    policy_row,
    ref_row,
    lengths_row,
    residual_grad,
    output_grad,
    gate_grad,
    up_grad,
    down_grad,
    context,
    residual,
    gate,
    up,
    upstream,
    gate_weight,
    up_weight,
    down_weight,
    weighted,
    normed,
    rms,
    partial,
    came_down,
    came_up,
    delta,
    gate_factor,
    up_factor,
    gate_delta,
    up_delta,
    down_total,
    row_products,
    share_out,
    share_in,
    normed_delta,
    other_half,
    dot_z,
    dot_plane,
    dot_column,
    grads,
    grad_groups,
    weight_out,
    weight_in,
    weight_own,
    load_sem,
    sum_sems,
    gather_sems,
    share_sems,
    spread_sems,
    other_sems,
    z_sems,
    plane_sems,
    weight_sems,
):
    n_dp, n_tensor, rows, hidden, features = size
    half_rows = rows // 2
    lane_tiles = hidden // 128
    chunk_tiles = partial.shape[0] // n_dp
    piece = chunk_tiles // PIECES
    ring_half = n_dp // 2
    groups = n_tensor // 2
    group_rows = half_rows // groups
    pair_rows = 2 * group_rows
    half_pairs = half_rows // pair_rows
    n_plane = 2 * n_tensor

    d = lax.axis_index("dp")
    s = lax.axis_index("segment")
    t = lax.axis_index("tensor")
    me = s * n_tensor + t
    row_base = s * half_rows
    own_cols = pl.ds(pl.multiple_of(s * 128, 128), 128)
    other_cols = pl.ds(pl.multiple_of((1 - s) * 128, 128), 128)

    def row_block(start, count):
        return pl.ds(pl.multiple_of(start, 16), count)

    loads = [
        pltpu.make_async_copy(source, target, load_sem.at[index])
        for index, (source, target) in enumerate(
            (
                (upstream_hbm, upstream),
                (down_weight_hbm, down_weight),
                (gate_hbm, gate),
                (up_hbm, up),
                (residual_hbm, residual),
                (gate_weight_hbm, gate_weight),
                (up_weight_hbm, up_weight),
                (context_hbm, context),
            )
        )
    ]
    for load in loads:
        load.start()

    barrier = pltpu.get_barrier_semaphore()

    def greet_z(i, carry):
        pl.semaphore_signal(
            barrier, inc=1, device_id=(wrapped(d + i, n_dp), s, t), device_id_type=MESH
        )
        return carry

    def plane_device(i):
        peer = wrapped(me + i, n_plane)
        return (d, peer // n_tensor, lax.rem(peer, n_tensor))

    def greet_plane(i, carry):
        pl.semaphore_signal(barrier, inc=1, device_id=plane_device(i), device_id_type=MESH)
        return carry

    lax.fori_loop(1, n_dp, greet_z, 0)
    lax.fori_loop(1, n_plane, greet_plane, 0)

    npo = 2.0 * jax.nn.sigmoid(0.1 * (policy_row[...] - ref_row[...]))
    valid = lengths_row[...] - (LEN - POS)
    sequences = npo.shape[1]
    loads[0].wait()

    def weigh(i, carry):
        start = i * 144
        row = lax.broadcasted_iota(jnp.int32, (144, sequences), 0) + start
        offset = row - POS * lax.broadcasted_iota(jnp.int32, (144, sequences), 1)
        keep = (offset >= 0) & (offset < POS) & (offset < valid)
        weight = jnp.sum(jnp.where(keep, npo, 0.0), axis=1, keepdims=True)
        block = row_block(start, 144)
        weighted[block, :] = (upstream[block, :].astype(F32) * weight).astype(BF16)
        return carry

    lax.fori_loop(0, rows // 144, weigh, 0)
    loads[1].wait()

    def first_product(i, carry):
        block = weighted[row_block(row_base + 64 * i, 64), :]
        product = dot_nt(block, down_weight[...])
        for r in range(4):
            for c in range(lane_tiles):
                partial[(4 * i + r) * lane_tiles + c] = product[
                    16 * r : 16 * r + 16, 128 * c : 128 * c + 128
                ].astype(BF16)
        return carry

    lax.fori_loop(0, half_rows // 64, first_product, 0)
    for tile in range(half_rows // 16 * lane_tiles, partial.shape[0]):
        partial[tile] = jnp.zeros((16, 128), BF16)

    def factor_block(i):
        block = row_block(i * 144, 144)
        source = row_block(row_base + i * 144, 144)
        gate_value = gate[source, :].astype(F32)
        up_value = up[source, :].astype(F32)
        squash = jax.nn.sigmoid(gate_value)
        gate_factor[block, :] = up_value * squash * (1.0 + gate_value * (1.0 - squash))
        up_factor[block, :] = gate_value * squash

    def hidden_block(i):
        block = row_block(i * 144, 144)
        gate_value = gate[block, :].astype(F32)
        up_value = up[block, :].astype(F32)
        value = (gate_value * jax.nn.sigmoid(gate_value) * up_value).astype(BF16)
        down_total[...] += dot_tn(value, weighted[block, own_cols])

    def norm_block(i):
        block = row_block(i * 128, 128)
        column = jnp.transpose(
            jnp.broadcast_to(rms_row[:, pl.ds(pl.multiple_of(i * 128, 128), 128)], (128, 128))
        )
        rms[block, :] = column
        for c in range(features // 128):
            cols = slice(128 * c, 128 * c + 128)
            normed[block, cols] = (
                residual[block, cols].astype(F32) * column * gain_row[:, cols]
            ).astype(BF16)

    down_total[...] = jnp.zeros(down_total.shape, F32)

    pl.semaphore_wait(barrier, n_dp - 1 + n_plane - 1)

    above = (wrapped(d + 1, n_dp), s, t)
    below = (wrapped(d - 1, n_dp), s, t)

    def tiles_of(chunk, p):
        return pl.ds(chunk * chunk_tiles + p * piece, piece)

    def sum_copy(source, buffer, way, j, p, target):
        return pltpu.make_async_remote_copy(
            src_ref=source,
            dst_ref=buffer.at[j, pl.ds(p * piece, piece)],
            send_sem=sum_sems.at[way, 0, j, p],
            recv_sem=sum_sems.at[way, 1, j, p],
            device_id=target,
            device_id_type=MESH,
        )

    def down_chunk(j):
        return wrapped(d - ring_half + j, n_dp)

    def up_chunk(j):
        return wrapped(d + ring_half - 1 - j, n_dp)

    ways = ((came_down, 0, below, down_chunk), (came_up, 1, above, up_chunk))

    def begin_sum(way, p):
        buffer, index, target, chunk_of = ways[way]
        sum_copy(partial.at[tiles_of(chunk_of(0), p)], buffer, index, 0, p, target).start()

    def step_sum(way, j, p):
        buffer, index, target, chunk_of = ways[way]
        here = pl.ds(p * piece, piece)
        held = buffer.at[j - 1, here]
        sum_copy(held, buffer, index, j - 1, p, target).wait_recv()
        own = partial[tiles_of(chunk_of(j), p)]
        buffer[j - 1, here] = (buffer[j - 1, here].astype(F32) + own.astype(F32)).astype(BF16)
        sum_copy(held, buffer, index, j, p, target).start()

    for p in range(PIECES):
        begin_sum(0, p)
        begin_sum(1, p)
    loads[2].wait()
    loads[3].wait()
    factor_steps = half_rows // 144

    def sum_step(j, carry):
        for p in range(PIECES):
            step_sum(0, j, p)
            step_sum(1, j, p)

        @pl.when(j <= factor_steps)
        def _():
            factor_block(j - 1)

        return carry

    lax.fori_loop(1, ring_half - 1, sum_step, 0)
    for i in range(ring_half - 2, factor_steps):
        factor_block(i)
    for p in range(PIECES):
        step_sum(0, ring_half - 1, p)
    loads[4].wait()

    def gather_copy(chunk, way, j, p, target):
        tiles = tiles_of(chunk, p)
        return pltpu.make_async_remote_copy(
            src_ref=delta.at[tiles],
            dst_ref=delta.at[tiles],
            send_sem=gather_sems.at[way, 0, j, p],
            recv_sem=gather_sems.at[way, 1, j, p],
            device_id=target,
            device_id_type=MESH,
        )

    for p in range(PIECES):
        here = pl.ds(p * piece, piece)
        sum_copy(came_down.at[ring_half - 1, here], came_down, 0, ring_half - 1, p, below).wait_recv()
        sum_copy(came_up.at[ring_half - 2, here], came_up, 1, ring_half - 2, p, above).wait_recv()
        delta[tiles_of(d, p)] = (
            came_down[ring_half - 1, here].astype(F32)
            + came_up[ring_half - 2, here].astype(F32)
            + partial[tiles_of(d, p)].astype(F32)
        ).astype(BF16)
        gather_copy(d, 0, 0, p, above).start()
        gather_copy(d, 1, 0, p, below).start()

    def step_gather(way, j, p):
        if way == 0:
            chunk, target = wrapped(d - j, n_dp), above
        else:
            chunk, target = wrapped(d + j, n_dp), below
        gather_copy(chunk, way, j - 1, p, target).wait_recv()
        gather_copy(chunk, way, j, p, target).start()

    hidden_steps = rows // 144
    norm_steps = rows // 128

    def gather_step(j, carry):
        for p in range(PIECES):
            step_gather(0, j, p)
            step_gather(1, j, p)
        hidden_block(j - 1)
        norm_block(j - 1)
        return carry

    lax.fori_loop(1, ring_half - 1, gather_step, 0)
    for p in range(PIECES):
        step_gather(0, ring_half - 1, p)
    lax.fori_loop(ring_half - 2, hidden_steps, lambda i, c: (hidden_block(i), c)[1], 0)
    lax.fori_loop(ring_half - 2, norm_steps, lambda i, c: (norm_block(i), c)[1], 0)
    down_grad[...] = down_total[...].astype(BF16)
    loads[5].wait()
    loads[6].wait()
    loads[7].wait()
    for p in range(PIECES):
        gather_copy(wrapped(d - ring_half, n_dp), 0, ring_half - 1, p, above).wait_recv()
        gather_copy(wrapped(d + ring_half - 1, n_dp), 1, ring_half - 2, p, below).wait_recv()

    def gate_block(i, carry):
        block = row_block(i * 16, 16)
        value = jnp.concatenate(
            [delta[i * lane_tiles + c] for c in range(lane_tiles)], axis=1
        ).astype(F32)
        gate_delta[block, :] = (value * gate_factor[block, :]).astype(BF16)
        up_delta[block, :] = (value * up_factor[block, :]).astype(BF16)
        return carry

    lax.fori_loop(0, half_rows // 16, gate_block, 0)

    def share_copy(slot, owner, source):
        return pltpu.make_async_remote_copy(
            src_ref=share_out.at[slot],
            dst_ref=share_in.at[source],
            send_sem=share_sems.at[0, slot],
            recv_sem=share_sems.at[1, source],
            device_id=(d, s, owner),
            device_id_type=MESH,
        )

    def share_block(i, carry):
        block = row_block(i * pair_rows, pair_rows)
        source = row_block(row_base + i * pair_rows, pair_rows)
        product = dot_nt(gate_delta[block, :], gate_weight[...]) + dot_nt(
            up_delta[block, :], up_weight[...]
        )
        for q in range(2):
            for c in range(2):
                owner = 4 * i + 2 * q + c
                share_out[owner] = product[
                    q * group_rows : (q + 1) * group_rows, 128 * c : 128 * c + 128
                ].astype(BF16)

                @pl.when(owner != t)
                def _():
                    share_copy(owner, owner, t).start()

                @pl.when(owner == t)
                def _():
                    share_in[t] = share_out[t]

        scaled = product * residual[source, :].astype(F32) * gain_row[...]
        row_products[block, :] = scaled[:, :128] + scaled[:, 128:]
        return carry

    row_products[half_rows:, :] = jnp.zeros((row_products.shape[0] - half_rows, 128), F32)
    lax.fori_loop(0, half_pairs, share_block, 0)

    def z_copy(slot, peer, source):
        return pltpu.make_async_remote_copy(
            src_ref=dot_z.at[d],
            dst_ref=dot_z.at[source],
            send_sem=z_sems.at[0, slot],
            recv_sem=z_sems.at[1, source],
            device_id=(peer, s, t),
            device_id_type=MESH,
        )

    for b in range(row_products.shape[0] // 128):
        cols = slice(128 * b, 128 * b + 128)
        dot_z[d, :, cols] = jnp.sum(jnp.transpose(row_products[cols, :]), axis=0, keepdims=True)

    def send_z(i, carry):
        z_copy(i, wrapped(d + i, n_dp), d).start()
        return carry

    lax.fori_loop(1, n_dp, send_z, 0)

    own_normed_rows = row_block(row_base, half_rows)
    partner = (d, 1 - s, t)

    def weight_copy(index):
        return pltpu.make_async_remote_copy(
            src_ref=weight_out.at[index],
            dst_ref=weight_in.at[index],
            send_sem=weight_sems.at[0, index],
            recv_sem=weight_sems.at[1, index],
            device_id=partner,
            device_id_type=MESH,
        )

    weight_out[0] = dot_tn(normed[own_normed_rows, other_cols], gate_delta[...]).astype(BF16)
    weight_copy(0).start()
    weight_out[1] = dot_tn(normed[own_normed_rows, other_cols], up_delta[...]).astype(BF16)
    weight_copy(1).start()

    def wait_share(i, carry):
        source = wrapped(t + i, n_tensor)
        share_copy(source, t, source).wait_recv()
        return carry

    lax.fori_loop(1, n_tensor, wait_share, 0)
    total = share_in[0].astype(F32)
    for k in range(1, n_tensor):
        total = total + share_in[k].astype(F32)
    own_group = s * groups + t // 2
    own_half = lax.rem(t, 2)
    share_out[t] = total.astype(BF16)

    def spread_copy(slot, peer, group):
        return pltpu.make_async_remote_copy(
            src_ref=share_out.at[t],
            dst_ref=normed_delta.at[group],
            send_sem=spread_sems.at[0, slot],
            recv_sem=spread_sems.at[1, group],
            device_id=(d, own_half, peer),
            device_id_type=MESH,
        )

    other_copy = pltpu.make_async_remote_copy(
        src_ref=share_out.at[t],
        dst_ref=other_half,
        send_sem=other_sems.at[0],
        recv_sem=other_sems.at[1],
        device_id=(d, 1 - own_half, own_group),
        device_id_type=MESH,
    )
    keeps = own_half == s
    other_here = (own_half != s) & (own_group == t)

    def send_spread(i, carry):
        spread_copy(i, wrapped(t + i, n_tensor), own_group).start()
        return carry

    lax.fori_loop(1, n_tensor, send_spread, 0)

    @pl.when(keeps)
    def _():
        normed_delta[own_group] = share_out[t]

    @pl.when(jnp.logical_not(keeps))
    def _():
        spread_copy(0, t, own_group).start()

    @pl.when(other_here)
    def _():
        other_half[...] = share_out[t]

    @pl.when(jnp.logical_not(other_here))
    def _():
        other_copy.start()

    def wait_z(i, carry):
        source = wrapped(d + i, n_dp)
        z_copy(i, source, source).wait_recv()
        return carry

    lax.fori_loop(1, n_dp, wait_z, 0)
    z_total = dot_z[0]
    for k in range(1, n_dp):
        z_total = z_total + dot_z[k]
    dot_plane[me] = z_total

    def plane_copy(i, source):
        return pltpu.make_async_remote_copy(
            src_ref=dot_plane.at[me],
            dst_ref=dot_plane.at[source],
            send_sem=plane_sems.at[0, i],
            recv_sem=plane_sems.at[1, source],
            device_id=plane_device(i),
            device_id_type=MESH,
        )

    def send_plane(i, carry):
        plane_copy(i, me).start()
        return carry

    lax.fori_loop(1, n_plane, send_plane, 0)

    weight_own[0] = dot_tn(normed[own_normed_rows, own_cols], gate_delta[...])
    weight_own[1] = dot_tn(normed[own_normed_rows, own_cols], up_delta[...])

    def wait_plane(i, carry):
        plane_copy(i, wrapped(me + i, n_plane)).wait_recv()
        return carry

    lax.fori_loop(1, n_plane, wait_plane, 0)
    for side in range(2):
        line = dot_plane[side * n_tensor]
        for k in range(1, n_tensor):
            line = line + dot_plane[side * n_tensor + k]
        for b in range(row_products.shape[0] // 128):
            cols = slice(128 * b, 128 * b + 128)
            dot_column[side, cols, :] = jnp.transpose(jnp.broadcast_to(line[:, cols], (128, 128)))

    def wait_spread(group, carry):
        side = group // groups
        owner = 2 * lax.rem(group, groups) + s

        @pl.when(jnp.logical_not((side == s) & (owner == t)))
        def _():
            spread_copy(0, t, group).wait_recv()

        return carry

    lax.fori_loop(0, n_tensor, wait_spread, 0)

    scale = 1.0 / (features * n_dp)

    def finish(weighted_value, residual_value, rms_value, gain_value, delta_value, dot_value):
        row_scale = rms_value * rms_value * rms_value * dot_value * scale
        return weighted_value + rms_value * gain_value * delta_value - residual_value * row_scale

    def finish_block(i, carry):
        block = row_block(i * pair_rows, pair_rows)
        side = i // half_pairs
        local = row_block((i - side * half_pairs) * pair_rows, pair_rows)
        value = finish(
            weighted[block, own_cols].astype(F32),
            residual[block, own_cols].astype(F32),
            rms[block, :],
            gain_row[:, own_cols],
            jnp.concatenate(
                [normed_delta[2 * i].astype(F32), normed_delta[2 * i + 1].astype(F32)], axis=0
            ),
            dot_column[side, local, :],
        )
        grads[block, :] = value.astype(BF16)
        grad_groups[2 * i] = value[:group_rows].astype(BF16)
        grad_groups[2 * i + 1] = value[group_rows:].astype(BF16)
        return carry

    lax.fori_loop(0, n_tensor // 2, finish_block, 0)
    output_grad[...] = dot_tn(context[...], grads[...]).astype(BF16)
    residual_grad[:, own_cols] = grad_groups[t]

    @pl.when(jnp.logical_not((t // groups == s) & (2 * lax.rem(t, groups) + 1 - s == t)))
    def _():
        other_copy.wait_recv()

    pair = t // 2
    pair_block = row_block(pair * pair_rows, pair_rows)
    pair_side = pair // half_pairs
    pair_local = row_block((pair - pair_side * half_pairs) * pair_rows, pair_rows)

    def own_rows(value):
        return jnp.where(own_half == 0, value[:group_rows], value[group_rows:])

    residual_grad[:, other_cols] = finish(
        own_rows(weighted[pair_block, other_cols].astype(F32)),
        own_rows(residual[pair_block, other_cols].astype(F32)),
        own_rows(rms[pair_block, :]),
        gain_row[:, other_cols],
        other_half[...].astype(F32),
        own_rows(dot_column[pair_side, pair_local, :]),
    ).astype(BF16)

    for index, target in enumerate((gate_grad, up_grad)):
        weight_copy(index).wait_recv()
        target[...] = (weight_own[index] + weight_in[index].astype(F32)).astype(BF16)

    def drain_ring(j, carry):
        for p in range(PIECES):
            here = pl.ds(p * piece, piece)
            sum_copy(came_down.at[0, here], came_down, 0, j, p, below).wait_send()
            gather_copy(d, 0, j, p, above).wait_send()

            @pl.when(j < ring_half - 1)
            def _():
                sum_copy(came_up.at[0, here], came_up, 1, j, p, above).wait_send()
                gather_copy(d, 1, j, p, below).wait_send()

        return carry

    lax.fori_loop(0, ring_half, drain_ring, 0)

    def drain_z(i, carry):
        z_copy(i, wrapped(d + i, n_dp), d).wait_send()
        return carry

    lax.fori_loop(1, n_dp, drain_z, 0)

    def drain_plane(i, carry):
        plane_copy(i, me).wait_send()
        return carry

    lax.fori_loop(1, n_plane, drain_plane, 0)

    def drain_share(i, carry):
        owner = wrapped(t + i, n_tensor)
        share_copy(owner, owner, t).wait_send()
        spread_copy(i, owner, own_group).wait_send()
        return carry

    lax.fori_loop(1, n_tensor, drain_share, 0)

    @pl.when(jnp.logical_not(keeps))
    def _():
        spread_copy(0, t, own_group).wait_send()

    @pl.when(jnp.logical_not(other_here))
    def _():
        other_copy.wait_send()

    for index in range(2):
        weight_copy(index).wait_send()


def shards(
    n_dp,
    n_tensor,
    context,
    residual,
    inverse_rms,
    norm_gain,
    gate_preact,
    up_preact,
    upstream,
    gate_weight,
    up_weight,
    down_weight,
    policy_logprob,
    ref_logprob,
    lengths,
):
    rows, features = residual.shape
    hidden = gate_preact.shape[1]
    half_rows = rows // 2
    groups = n_tensor // 2
    group_rows = half_rows // groups
    tiles = half_rows // 16 * (hidden // 128)
    chunk_tiles = -(-tiles // (n_dp * PIECES)) * PIECES
    ring_half = n_dp // 2
    padded = -(-half_rows // 128) * 128
    vmem = pl.BlockSpec(memory_space=pltpu.VMEM)
    hbm = pl.BlockSpec(memory_space=pl.ANY)

    def like(array):
        return pltpu.VMEM(array.shape, array.dtype)

    dma = pltpu.SemaphoreType.DMA
    size = (n_dp, n_tensor, rows, hidden, features)
    return pl.pallas_call(
        functools.partial(kernel, size),
        out_shape=(
            jax.ShapeDtypeStruct((rows // n_tensor, features), BF16),
            jax.ShapeDtypeStruct((context.shape[1], features // 2), BF16),
            jax.ShapeDtypeStruct((features // 2, hidden), BF16),
            jax.ShapeDtypeStruct((features // 2, hidden), BF16),
            jax.ShapeDtypeStruct((hidden, features // 2), BF16),
        ),
        in_specs=[hbm, hbm, vmem, vmem, hbm, hbm, hbm, hbm, hbm, hbm, vmem, vmem, vmem],
        out_specs=(vmem,) * 5,
        scratch_shapes=[
            like(context),
            like(residual),
            like(gate_preact),
            like(up_preact),
            like(upstream),
            like(gate_weight),
            like(up_weight),
            like(down_weight),
            pltpu.VMEM((rows, features), BF16),
            pltpu.VMEM((rows, features), BF16),
            pltpu.VMEM((rows, 128), F32),
            pltpu.VMEM((n_dp * chunk_tiles, 16, 128), BF16),
            pltpu.VMEM((ring_half, chunk_tiles, 16, 128), BF16),
            pltpu.VMEM((ring_half, chunk_tiles, 16, 128), BF16),
            pltpu.VMEM((n_dp * chunk_tiles, 16, 128), BF16),
            pltpu.VMEM((half_rows, hidden), F32),
            pltpu.VMEM((half_rows, hidden), F32),
            pltpu.VMEM((half_rows, hidden), BF16),
            pltpu.VMEM((half_rows, hidden), BF16),
            pltpu.VMEM((hidden, features // 2), F32),
            pltpu.VMEM((padded, 128), F32),
            pltpu.VMEM((n_tensor, group_rows, 128), BF16),
            pltpu.VMEM((n_tensor, group_rows, 128), BF16),
            pltpu.VMEM((n_tensor, group_rows, 128), BF16),
            pltpu.VMEM((group_rows, 128), BF16),
            pltpu.VMEM((n_dp, 1, padded), F32),
            pltpu.VMEM((2 * n_tensor, 1, padded), F32),
            pltpu.VMEM((2, padded, 128), F32),
            pltpu.VMEM((rows, 128), BF16),
            pltpu.VMEM((n_tensor, group_rows, 128), BF16),
            pltpu.VMEM((2, features // 2, hidden), BF16),
            pltpu.VMEM((2, features // 2, hidden), BF16),
            pltpu.VMEM((2, features // 2, hidden), F32),
            dma((8,)),
            dma((2, 2, ring_half, PIECES)),
            dma((2, 2, ring_half, PIECES)),
            dma((2, n_tensor)),
            dma((2, n_tensor)),
            dma((2,)),
            dma((2, n_dp)),
            dma((2, 2 * n_tensor)),
            dma((2, 2)),
        ],
        compiler_params=pltpu.CompilerParams(
            collective_id=0, has_side_effects=True, vmem_limit_bytes=48 * 1024 * 1024
        ),
    )(
        context,
        residual,
        inverse_rms.reshape(1, -1),
        norm_gain.reshape(1, -1),
        gate_preact,
        up_preact,
        upstream,
        gate_weight,
        up_weight,
        down_weight,
        policy_logprob.reshape(1, -1),
        ref_logprob.reshape(1, -1),
        lengths.reshape(1, -1),
    )


def solution(mesh):
    return jax.shard_map(
        functools.partial(shards, mesh.shape["dp"], mesh.shape["tensor"]),
        mesh=mesh,
        in_specs=(
            P(None, "tensor"),
            P(None, "dp"),
            P(),
            P("dp"),
            P(None, "tensor"),
            P(None, "tensor"),
            P(None, "dp"),
            P("dp", "tensor"),
            P("dp", "tensor"),
            P("tensor", "dp"),
            P(),
            P(),
            P(),
        ),
        out_specs=(
            P("tensor", "dp"),
            P("tensor", ("dp", "segment")),
            P(("dp", "segment"), "tensor"),
            P(("dp", "segment"), "tensor"),
            P("tensor", ("dp", "segment")),
        ),
        check_vma=False,
    )
```

time: 376 us -> 106 us (0.28)
  waiting for transfers between devices: 282 us -> 0 us
  Pallas kernels: 0 us -> 90 us
  blocking collectives: 30.8 us -> 0 us
  starting transfers between devices: 26.1 us -> 0 us
  other arithmetic: 16.6 us -> 0 us
  between operations: 14.3 us -> 0.65 us
  local copies, waits for them, and re-layouts: 4.94 us -> 14.5 us
    psum x2 -> x0, waiting for transfers between devices: 265 us -> none  [the longest x1 150 us: shards(): lax.psum(lax.cond(ffn_side, lambda: jnp.einsum('td,fd->tf', weighted, dow...]
    pallas_call x0 -> x1, Pallas kernels: none -> 90 us  [shards(): pl.pallas_call(functools.partial(kernel, size), out_shape=(jax.ShapeDtype...]
    psum x1 -> x0, blocking collectives: 30.8 us -> none  [row_statistic(): return lax.psum(partial_dot, 'dp')]
    ppermute x5 -> x0, starting transfers between devices: 26 us -> none  [the longest x4 24.6 us: from_partner(): return lax.ppermute(value, axis, pairs)]
    ppermute x5 -> x0, waiting for transfers between devices: 16.7 us -> none  [the longest x4 16.7 us: from_partner(): return lax.ppermute(value, axis, pairs)]
    unnamed x18 -> x27, local copies, waits for them, and re-layouts: 2.17 us -> 13.8 us
    convert_element_type x3 -> x0, other arithmetic: 9.74 us -> none  [the longest x1 5.76 us: shards(): (gate_value * jax.nn.sigmoid(gate_value) * up_value).astype(jnp.bfloat16)]
    select_n x7 -> x0, other arithmetic: 3.93 us -> none  [the longest x1 1.77 us: shards(): down_weight_grad = jnp.where(ffn_side, down_bf[:, half_width:], got_down)]
  transfers between devices with their start and end apart: 7 -> 0, of which waited for: 4 -> 0; matrix products, arithmetic and copies ran while one was open for 3% -> 0% of each run, Pallas kernels for 0% -> 0%
where the time goes in v1:
time: 106 us; the launch traced here: 105 us
  Pallas kernels  90 us (85%)
  local copies, waits for them, and re-layouts  14.5 us (14%)
    pallas_call x1, Pallas kernels, shards(): pl.pallas_call(functools.partial(kernel, size), out_shape=(jax.ShapeDtype...  90 us
    unnamed x27, local copies, waits for them, and re-layouts  13.8 us

profile of v1, /device:TPU:6, one launch (start us, length us, event | category | flops | bytes accessed | tf_op | source)
XLA Modules:
  0.0 105.2 jit_solution(255621045406895389)
XLA Ops:
  0.6 0.7 reshape.25.rms_row
  1.3 0.0 copy-start
  1.3 1.6 %copy-done = bf16[1152,896]{1,0:T(8,128)(2,1)S(1)} copy-done((bf16[1152,896]{1,0:T(8,128)(2,1)S(1)}, bf16[1152,896]{1,0:T(8,128)(2,1)}, u32[]{:S(2)}) %copy-start) | copy-done | bytes 2064408
  2.9 0.0 copy-start.1
  2.9 1.1 %copy-done.1 = bf16[1152,256]{1,0:T(8,128)(2,1)S(1)} copy-done((bf16[1152,256]{1,0:T(8,128)(2,1)S(1)}, bf16[1152,256]{1,0:T(8,128)(2,1)}, u32[]{:S(2)}) %copy-start.1) | copy-done | bytes 589848
  4.0 0.0 copy-start.2
  4.0 1.1 %copy-done.2 = bf16[1152,256]{1,0:T(8,128)(2,1)S(1)} copy-done((bf16[1152,256]{1,0:T(8,128)(2,1)S(1)}, bf16[1152,256]{1,0:T(8,128)(2,1)}, u32[]{:S(2)}) %copy-start.2) | copy-done | bytes 589848
  5.0 0.0 copy-start.3
  5.0 1.1 %copy-done.3 = bf16[1152,256]{1,0:T(8,128)(2,1)S(1)} copy-done((bf16[1152,256]{1,0:T(8,128)(2,1)S(1)}, bf16[1152,256]{1,0:T(8,128)(2,1)}, u32[]{:S(2)}) %copy-start.3) | copy-done | bytes 589848
  6.1 0.0 copy-start.4
  6.1 1.0 copy-done.4
  7.1 0.0 copy-start.5
  7.1 1.0 copy-done.5
  8.1 0.0 copy-start.6
  8.1 1.0 copy-done.6
  9.2 0.0 copy-start.7
  9.2 0.7 copy-done.7
  9.8 0.0 copy-start.8
  9.8 0.7 copy-done.8
  10.5 0.0 copy-start.9
  10.5 0.7 copy-done.9
  11.2 0.0 copy-start.10
  11.2 0.7 copy-done.10
  11.8 90.0 %shard_map.164 = (bf16[72,256]{1,0:T(8,128)(2,1)S(1)}, bf16[256,128]{1,0:T(8,128)(2,1)S(1)}, bf16[128,896]{1,0:T(8,128)(2,1)S(1)}, bf16[128,896]{1,0:T(8,128)(2,1)S(1)}, bf16[896,128]{1,0:T(8,128)(2,1)S(1)}) custom-call(bf16[1152,256]{1,0:T(8,128)(2,1)S(1)} %copy-done.1, bf16[1152,256]{1,0:T(8,128)(2,1)S(1)} %copy-done.2, f32[1,1152]{1,0:T(1,128)S(1)} %reshape.25.rms_row, ...), custom_call_target="tpu_custom_call" | custom-call | tf_op jit(solution)/shard_map/pallas_call | solution.py:668
  101.9 0.6 copy.23
  102.5 0.6 copy.24
  103.1 0.7 copy.25
  103.8 0.7 copy.26
  104.5 0.7 copy.27
Async XLA Ops:
  1.3 1.6 %copy-start = (bf16[1152,896]{1,0:T(8,128)(2,1)S(1)}, bf16[1152,896]{1,0:T(8,128)(2,1)}, u32[]{:S(2)}) copy-start(bf16[1152,896]{1,0:T(8,128)(2,1)} %gate_hbm.1) | copy-start | bytes 6193156
  2.9 1.1 %copy-start.1 = (bf16[1152,256]{1,0:T(8,128)(2,1)S(1)}, bf16[1152,256]{1,0:T(8,128)(2,1)}, u32[]{:S(2)}) copy-start(bf16[1152,256]{1,0:T(8,128)(2,1)} %context_hbm.1) | copy-start | bytes 1769476
  4.0 1.1 %copy-start.2 = (bf16[1152,256]{1,0:T(8,128)(2,1)S(1)}, bf16[1152,256]{1,0:T(8,128)(2,1)}, u32[]{:S(2)}) copy-start(bf16[1152,256]{1,0:T(8,128)(2,1)} %residual_hbm.1) | copy-start | bytes 1769476
  5.0 1.1 %copy-start.3 = (bf16[1152,256]{1,0:T(8,128)(2,1)S(1)}, bf16[1152,256]{1,0:T(8,128)(2,1)}, u32[]{:S(2)}) copy-start(bf16[1152,256]{1,0:T(8,128)(2,1)} %upstream_hbm.1) | copy-start | bytes 1769476
  6.1 1.0 copy-start.4
  7.1 1.0 copy-start.5
  8.1 1.0 copy-start.6
  9.2 0.7 copy-start.7
  9.8 0.7 copy-start.8
  10.5 0.7 copy-start.9
  11.2 0.7 copy-start.10

commit v2 on v1

--- a/solution.py
+++ b/solution.py
@@ -10,7 +10,10 @@
 
 POS = 36
 LEN = 4096
-PIECES = 4
+PIECES = 2
+HIDDEN_EARLY = 3
+PLACES = (8, 7, 3, 6, 4, -8, -7, -3, -6, -4, 2, -2, 1, -1)
+RELAYS = (5, -5)
 MESH = pl.DeviceIdType.MESH
 BF16 = jnp.bfloat16
 F32 = jnp.float32
@@ -18,6 +21,18 @@
 
 def wrapped(value, count):
     return lax.rem(value + count, count)
+
+
+def relay_of(place):
+    if abs(place) < 3:
+        return 0
+    return 5 if place > 0 else -5
+
+
+def goes(place, piece):
+    if abs(place) < 8:
+        return True
+    return (place > 0) == (piece < PIECES // 2)
 
 
 def dot_nt(a, b):
@@ -32,7 +47,7 @@
     size,
     context_hbm,
     residual_hbm,
-    rms_row,
+    rms_hbm,
     gain_row,
     gate_hbm,
     up_hbm,
@@ -58,10 +73,11 @@
     down_weight,
     weighted,
     normed,
+    rms_row,
     rms,
     partial,
-    came_down,
-    came_up,
+    arrived,
+    relayed,
     delta,
     gate_factor,
     up_factor,
@@ -96,7 +112,6 @@
     lane_tiles = hidden // 128
     chunk_tiles = partial.shape[0] // n_dp
     piece = chunk_tiles // PIECES
-    ring_half = n_dp // 2
     groups = n_tensor // 2
     group_rows = half_rows // groups
     pair_rows = 2 * group_rows
@@ -126,6 +141,7 @@
                 (gate_weight_hbm, gate_weight),
                 (up_weight_hbm, up_weight),
                 (context_hbm, context),
+                (rms_hbm, rms_row.at[0]),
             )
         )
     ]
@@ -148,7 +164,9 @@
         pl.semaphore_signal(barrier, inc=1, device_id=plane_device(i), device_id_type=MESH)
         return carry
 
-    lax.fori_loop(1, n_dp, greet_z, 0)
+    for offset in (1, 2, 3):
+        greet_z(offset, 0)
+        greet_z(-offset, 0)
     lax.fori_loop(1, n_plane, greet_plane, 0)
 
     npo = 2.0 * jax.nn.sigmoid(0.1 * (policy_row[...] - ref_row[...]))
@@ -213,124 +231,112 @@
 
     down_total[...] = jnp.zeros(down_total.shape, F32)
 
-    pl.semaphore_wait(barrier, n_dp - 1 + n_plane - 1)
-
-    above = (wrapped(d + 1, n_dp), s, t)
-    below = (wrapped(d - 1, n_dp), s, t)
+    pl.semaphore_wait(barrier, 6 + n_plane - 1)
+
+    def at_z(offset):
+        return (wrapped(d + offset, n_dp), s, t)
 
     def tiles_of(chunk, p):
         return pl.ds(chunk * chunk_tiles + p * piece, piece)
 
-    def sum_copy(source, buffer, way, j, p, target):
+    def sum_copy(slot, p, source, target):
         return pltpu.make_async_remote_copy(
             src_ref=source,
-            dst_ref=buffer.at[j, pl.ds(p * piece, piece)],
-            send_sem=sum_sems.at[way, 0, j, p],
-            recv_sem=sum_sems.at[way, 1, j, p],
+            dst_ref=arrived.at[slot, pl.ds(p * piece, piece)],
+            send_sem=sum_sems.at[0, slot, p],
+            recv_sem=sum_sems.at[1, slot, p],
             device_id=target,
             device_id_type=MESH,
         )
 
-    def down_chunk(j):
-        return wrapped(d - ring_half + j, n_dp)
-
-    def up_chunk(j):
-        return wrapped(d + ring_half - 1 - j, n_dp)
-
-    ways = ((came_down, 0, below, down_chunk), (came_up, 1, above, up_chunk))
-
-    def begin_sum(way, p):
-        buffer, index, target, chunk_of = ways[way]
-        sum_copy(partial.at[tiles_of(chunk_of(0), p)], buffer, index, 0, p, target).start()
-
-    def step_sum(way, j, p):
-        buffer, index, target, chunk_of = ways[way]
+    def own_sum_copy(slot, p):
+        place = PLACES[slot]
+        return sum_copy(
+            slot, p, partial.at[tiles_of(wrapped(d - place, n_dp), p)], at_z(relay_of(place) - place)
+        )
+
+    def relay_sum_copy(index, p):
+        held = relayed.at[index, pl.ds(p * piece, piece)]
+        return sum_copy(len(PLACES) + index, p, held, at_z(-RELAYS[index]))
+
+    def added(chunk, slots, p):
         here = pl.ds(p * piece, piece)
-        held = buffer.at[j - 1, here]
-        sum_copy(held, buffer, index, j - 1, p, target).wait_recv()
-        own = partial[tiles_of(chunk_of(j), p)]
-        buffer[j - 1, here] = (buffer[j - 1, here].astype(F32) + own.astype(F32)).astype(BF16)
-        sum_copy(held, buffer, index, j, p, target).start()
-
+        value = partial[tiles_of(chunk, p)].astype(F32)
+        for slot in slots:
+            sum_copy(slot, p, partial.at[here], below).wait_recv()
+            value = value + arrived[slot, here].astype(F32)
+        return value.astype(BF16)
+
+    below = at_z(-1)
     for p in range(PIECES):
-        begin_sum(0, p)
-        begin_sum(1, p)
+        for slot, place in enumerate(PLACES):
+            if relay_of(place) and goes(place, p):
+                own_sum_copy(slot, p).start()
+    for p in range(PIECES):
+        for slot, place in enumerate(PLACES):
+            if not relay_of(place):
+                own_sum_copy(slot, p).start()
     loads[2].wait()
     loads[3].wait()
-    factor_steps = half_rows // 144
-
-    def sum_step(j, carry):
-        for p in range(PIECES):
-            step_sum(0, j, p)
-            step_sum(1, j, p)
-
-        @pl.when(j <= factor_steps)
-        def _():
-            factor_block(j - 1)
-
-        return carry
-
-    lax.fori_loop(1, ring_half - 1, sum_step, 0)
-    for i in range(ring_half - 2, factor_steps):
-        factor_block(i)
+    lax.fori_loop(0, half_rows // 144, lambda i, c: (factor_block(i), c)[1], 0)
     for p in range(PIECES):
-        step_sum(0, ring_half - 1, p)
-    loads[4].wait()
-
-    def gather_copy(chunk, way, j, p, target):
+        for index, relay in enumerate(RELAYS):
+            slots = [
+                slot
+                for slot, place in enumerate(PLACES)
+                if relay_of(place) == relay and goes(place, p)
+            ]
+            relayed[index, pl.ds(p * piece, piece)] = added(wrapped(d - relay, n_dp), slots, p)
+            relay_sum_copy(index, p).start()
+    lax.fori_loop(0, HIDDEN_EARLY, lambda i, c: (hidden_block(i), c)[1], 0)
+
+    def gather_copy(kind, chunk, p, target):
         tiles = tiles_of(chunk, p)
         return pltpu.make_async_remote_copy(
             src_ref=delta.at[tiles],
             dst_ref=delta.at[tiles],
-            send_sem=gather_sems.at[way, 0, j, p],
-            recv_sem=gather_sems.at[way, 1, j, p],
+            send_sem=gather_sems.at[0, kind, p],
+            recv_sem=gather_sems.at[1, kind, p],
             device_id=target,
             device_id_type=MESH,
         )
 
+    def source_copy(kind, p):
+        step = RELAYS[kind - len(PLACES)] if kind >= len(PLACES) else PLACES[kind]
+        return gather_copy(kind, d, p, at_z(step))
+
+    def relay_copy(kind, p):
+        place = PLACES[kind]
+        relay = relay_of(place)
+        return gather_copy(kind, wrapped(d - relay, n_dp), p, at_z(place - relay))
+
+    near = [slot for slot, place in enumerate(PLACES) if not relay_of(place)]
+    far = [len(PLACES) + index for index in range(len(RELAYS))]
     for p in range(PIECES):
-        here = pl.ds(p * piece, piece)
-        sum_copy(came_down.at[ring_half - 1, here], came_down, 0, ring_half - 1, p, below).wait_recv()
-        sum_copy(came_up.at[ring_half - 2, here], came_up, 1, ring_half - 2, p, above).wait_recv()
-        delta[tiles_of(d, p)] = (
-            came_down[ring_half - 1, here].astype(F32)
-            + came_up[ring_half - 2, here].astype(F32)
-            + partial[tiles_of(d, p)].astype(F32)
-        ).astype(BF16)
-        gather_copy(d, 0, 0, p, above).start()
-        gather_copy(d, 1, 0, p, below).start()
-
-    def step_gather(way, j, p):
-        if way == 0:
-            chunk, target = wrapped(d - j, n_dp), above
-        else:
-            chunk, target = wrapped(d + j, n_dp), below
-        gather_copy(chunk, way, j - 1, p, target).wait_recv()
-        gather_copy(chunk, way, j, p, target).start()
-
-    hidden_steps = rows // 144
-    norm_steps = rows // 128
-
-    def gather_step(j, carry):
-        for p in range(PIECES):
-            step_gather(0, j, p)
-            step_gather(1, j, p)
-        hidden_block(j - 1)
-        norm_block(j - 1)
-        return carry
-
-    lax.fori_loop(1, ring_half - 1, gather_step, 0)
+        delta[tiles_of(d, p)] = added(d, near + far, p)
+        for kind in far:
+            source_copy(kind, p).start()
     for p in range(PIECES):
-        step_gather(0, ring_half - 1, p)
-    lax.fori_loop(ring_half - 2, hidden_steps, lambda i, c: (hidden_block(i), c)[1], 0)
-    lax.fori_loop(ring_half - 2, norm_steps, lambda i, c: (norm_block(i), c)[1], 0)
+        for kind in near:
+            source_copy(kind, p).start()
+    loads[4].wait()
+    loads[8].wait()
+    lax.fori_loop(0, rows // 128, lambda i, c: (norm_block(i), c)[1], 0)
+    for p in range(PIECES):
+        for index, relay in enumerate(RELAYS):
+            source_copy(far[index], p).wait_recv()
+            for kind, place in enumerate(PLACES):
+                if relay_of(place) == relay and goes(place, p):
+                    relay_copy(kind, p).start()
+    lax.fori_loop(HIDDEN_EARLY, rows // 144, lambda i, c: (hidden_block(i), c)[1], 0)
     down_grad[...] = down_total[...].astype(BF16)
     loads[5].wait()
     loads[6].wait()
     loads[7].wait()
     for p in range(PIECES):
-        gather_copy(wrapped(d - ring_half, n_dp), 0, ring_half - 1, p, above).wait_recv()
-        gather_copy(wrapped(d + ring_half - 1, n_dp), 1, ring_half - 2, p, below).wait_recv()
+        for kind, place in enumerate(PLACES):
+            if goes(place, p):
+                gather_copy(kind, d, p, below).wait_recv()
 
     def gate_block(i, carry):
         block = row_block(i * 16, 16)
@@ -584,20 +590,11 @@
         weight_copy(index).wait_recv()
         target[...] = (weight_own[index] + weight_in[index].astype(F32)).astype(BF16)
 
-    def drain_ring(j, carry):
-        for p in range(PIECES):
-            here = pl.ds(p * piece, piece)
-            sum_copy(came_down.at[0, here], came_down, 0, j, p, below).wait_send()
-            gather_copy(d, 0, j, p, above).wait_send()
-
-            @pl.when(j < ring_half - 1)
-            def _():
-                sum_copy(came_up.at[0, here], came_up, 1, j, p, above).wait_send()
-                gather_copy(d, 1, j, p, below).wait_send()
-
-        return carry
-
-    lax.fori_loop(0, ring_half, drain_ring, 0)
+    for p in range(PIECES):
+        for kind in range(len(PLACES) + len(RELAYS)):
+            if kind in far or goes(PLACES[kind], p):
+                sum_copy(kind, p, partial.at[tiles_of(d, p)], below).wait_send()
+                gather_copy(kind, d, p, below).wait_send()
 
     def drain_z(i, carry):
         z_copy(i, wrapped(d + i, n_dp), d).wait_send()
@@ -629,6 +626,18 @@
 
     for index in range(2):
         weight_copy(index).wait_send()
+
+
+def hand_on(*refs):
+    count = len(refs) // 2
+    sems = refs[-1]
+    copies = [
+        pltpu.make_async_copy(refs[i], refs[count + i], sems.at[i]) for i in range(count)
+    ]
+    for copy in copies:
+        copy.start()
+    for copy in copies:
+        copy.wait()
 
 
 def shards(
@@ -655,7 +664,7 @@
     group_rows = half_rows // groups
     tiles = half_rows // 16 * (hidden // 128)
     chunk_tiles = -(-tiles // (n_dp * PIECES)) * PIECES
-    ring_half = n_dp // 2
+    ways = len(PLACES) + len(RELAYS)
     padded = -(-half_rows // 128) * 128
     vmem = pl.BlockSpec(memory_space=pltpu.VMEM)
     hbm = pl.BlockSpec(memory_space=pl.ANY)
@@ -665,16 +674,17 @@
 
     dma = pltpu.SemaphoreType.DMA
     size = (n_dp, n_tensor, rows, hidden, features)
-    return pl.pallas_call(
-        functools.partial(kernel, size),
-        out_shape=(
+    out_shape = (
             jax.ShapeDtypeStruct((rows // n_tensor, features), BF16),
             jax.ShapeDtypeStruct((context.shape[1], features // 2), BF16),
             jax.ShapeDtypeStruct((features // 2, hidden), BF16),
             jax.ShapeDtypeStruct((features // 2, hidden), BF16),
             jax.ShapeDtypeStruct((hidden, features // 2), BF16),
-        ),
-        in_specs=[hbm, hbm, vmem, vmem, hbm, hbm, hbm, hbm, hbm, hbm, vmem, vmem, vmem],
+    )
+    grads = pl.pallas_call(
+        functools.partial(kernel, size),
+        out_shape=out_shape,
+        in_specs=[hbm, hbm, hbm, vmem, hbm, hbm, hbm, hbm, hbm, hbm, vmem, vmem, vmem],
         out_specs=(vmem,) * 5,
         scratch_shapes=[
             like(context),
@@ -687,10 +697,11 @@
             like(down_weight),
             pltpu.VMEM((rows, features), BF16),
             pltpu.VMEM((rows, features), BF16),
+            pltpu.VMEM((1, rows), F32),
             pltpu.VMEM((rows, 128), F32),
             pltpu.VMEM((n_dp * chunk_tiles, 16, 128), BF16),
-            pltpu.VMEM((ring_half, chunk_tiles, 16, 128), BF16),
-            pltpu.VMEM((ring_half, chunk_tiles, 16, 128), BF16),
+            pltpu.VMEM((ways, chunk_tiles, 16, 128), BF16),
+            pltpu.VMEM((len(RELAYS), chunk_tiles, 16, 128), BF16),
             pltpu.VMEM((n_dp * chunk_tiles, 16, 128), BF16),
             pltpu.VMEM((half_rows, hidden), F32),
             pltpu.VMEM((half_rows, hidden), F32),
@@ -710,9 +721,9 @@
             pltpu.VMEM((2, features // 2, hidden), BF16),
             pltpu.VMEM((2, features // 2, hidden), BF16),
             pltpu.VMEM((2, features // 2, hidden), F32),
-            dma((8,)),
-            dma((2, 2, ring_half, PIECES)),
-            dma((2, 2, ring_half, PIECES)),
+            dma((9,)),
+            dma((2, ways, PIECES)),
+            dma((2, ways, PIECES)),
             dma((2, n_tensor)),
             dma((2, n_tensor)),
             dma((2,)),
@@ -721,12 +732,12 @@
             dma((2, 2)),
         ],
         compiler_params=pltpu.CompilerParams(
-            collective_id=0, has_side_effects=True, vmem_limit_bytes=48 * 1024 * 1024
+            collective_id=0, has_side_effects=True, vmem_limit_bytes=63 * 1024 * 1024
         ),
     )(
         context,
         residual,
-        inverse_rms.reshape(1, -1),
+        inverse_rms,
         norm_gain.reshape(1, -1),
         gate_preact,
         up_preact,
@@ -738,6 +749,13 @@
         ref_logprob.reshape(1, -1),
         lengths.reshape(1, -1),
     )
+    return pl.pallas_call(
+        hand_on,
+        out_shape=out_shape,
+        in_specs=[hbm] * 5,
+        out_specs=(hbm,) * 5,
+        scratch_shapes=[dma((5,))],
+    )(*grads)
 
 
 def solution(mesh):

time: 106 us -> 114 us (1.075)
  Pallas kernels: 90 us -> 113 us
  local copies, waits for them, and re-layouts: 14.5 us -> 0 us
    pallas_call x1 -> x2, Pallas kernels: 90 us -> 113 us  [the longest x1 87.7 us: shards(): pl.pallas_call(functools.partial(kernel, size), out_shape=out_shape, in_s...]
    unnamed x27 -> x0, local copies, waits for them, and re-layouts: 13.8 us -> none
where the time goes in v2:
time: 114 us; the launch traced here: 113 us
  Pallas kernels  113 us (99%)
    pallas_call x1, Pallas kernels, shards(): pl.pallas_call(functools.partial(kernel, size), out_shape=out_shape, in_s...  87.7 us
    pallas_call x1, Pallas kernels, shards(): pl.pallas_call(hand_on, out_shape=out_shape, in_specs=[hbm] * 5, out_spec...  25.1 us

profile of v2, /device:TPU:6, one launch (start us, length us, event | category | flops | bytes accessed | tf_op | source)
XLA Modules:
  0.0 113.4 jit_solution(9490288029699843455)
XLA Ops:
  0.6 87.7 %shard_map.164 = (bf16[72,256]{1,0:T(8,128)(2,1)}, bf16[256,128]{1,0:T(8,128)(2,1)}, bf16[128,896]{1,0:T(8,128)(2,1)}, bf16[128,896]{1,0:T(8,128)(2,1)}, bf16[896,128]{1,0:T(8,128)(2,1)}) custom-call(bf16[1152,256]{1,0:T(8,128)(2,1)} %context_hbm.1, bf16[1152,256]{1,0:T(8,128)(2,1)} %residual_hbm.1, f32[1152]{0:T(1024)} %rms_hbm.1, f32[1,256]{1,0:T(1,128)} %bitcast.4, ...), custom_call_target="tpu_custom_call" | custom-call | tf_op jit(solution)/shard_map/pallas_call | solution.py:684
  88.3 25.1 %shard_map.165 = (bf16[72,256]{1,0:T(8,128)(2,1)}, bf16[256,128]{1,0:T(8,128)(2,1)}, bf16[128,896]{1,0:T(8,128)(2,1)}, bf16[128,896]{1,0:T(8,128)(2,1)}, bf16[896,128]{1,0:T(8,128)(2,1)}) custom-call(bf16[72,256]{1,0:T(8,128)(2,1)} %get-tuple-element.10.refs_0_, bf16[256,128]{1,0:T(8,128)(2,1)} %get-tuple-element.11.refs_1_, ...), custom_call_target="tpu_custom_call" | custom-call | tf_op jit(solution)/shard_map/pallas_call | solution.py:752

commit v3 on v2

--- a/solution.py
+++ b/solution.py
@@ -10,10 +10,9 @@
 
 POS = 36
 LEN = 4096
-PIECES = 2
-HIDDEN_EARLY = 3
-PLACES = (8, 7, 3, 6, 4, -8, -7, -3, -6, -4, 2, -2, 1, -1)
-RELAYS = (5, -5)
+PIECES = 4
+PLACES = (8, -8, 7, -7, 6, -6, 5, -5, 4, -4, 3, -3, 2, -2, 1, -1)
+CHAIN = (8, 6, 4, 2, 0)
 MESH = pl.DeviceIdType.MESH
 BF16 = jnp.bfloat16
 F32 = jnp.float32
@@ -23,16 +22,19 @@
     return lax.rem(value + count, count)
 
 
-def relay_of(place):
-    if abs(place) < 3:
-        return 0
-    return 5 if place > 0 else -5
+def inward(place):
+    below = max(c for c in CHAIN if c < abs(place))
+    return below if place > 0 else -below
 
 
 def goes(place, piece):
     if abs(place) < 8:
         return True
     return (place > 0) == (piece < PIECES // 2)
+
+
+def feeders(place, piece):
+    return [q for q in PLACES if inward(q) == place and goes(q, piece)]
 
 
 def dot_nt(a, b):
@@ -239,104 +241,88 @@
     def tiles_of(chunk, p):
         return pl.ds(chunk * chunk_tiles + p * piece, piece)
 
-    def sum_copy(slot, p, source, target):
+    def sum_copy(place, p):
+        chunk = wrapped(d - place, n_dp)
+        here = pl.ds(p * piece, piece)
+        slot = PLACES.index(place)
+        held = relayed.at[slot, here] if feeders(place, p) else partial.at[tiles_of(chunk, p)]
         return pltpu.make_async_remote_copy(
-            src_ref=source,
-            dst_ref=arrived.at[slot, pl.ds(p * piece, piece)],
+            src_ref=held,
+            dst_ref=arrived.at[slot, here],
             send_sem=sum_sems.at[0, slot, p],
             recv_sem=sum_sems.at[1, slot, p],
-            device_id=target,
+            device_id=at_z(inward(place) - place),
             device_id_type=MESH,
         )
 
-    def own_sum_copy(slot, p):
-        place = PLACES[slot]
-        return sum_copy(
-            slot, p, partial.at[tiles_of(wrapped(d - place, n_dp), p)], at_z(relay_of(place) - place)
-        )
-
-    def relay_sum_copy(index, p):
-        held = relayed.at[index, pl.ds(p * piece, piece)]
-        return sum_copy(len(PLACES) + index, p, held, at_z(-RELAYS[index]))
-
-    def added(chunk, slots, p):
+    def added(place, p):
         here = pl.ds(p * piece, piece)
-        value = partial[tiles_of(chunk, p)].astype(F32)
-        for slot in slots:
-            sum_copy(slot, p, partial.at[here], below).wait_recv()
-            value = value + arrived[slot, here].astype(F32)
+        value = partial[tiles_of(wrapped(d - place, n_dp), p)].astype(F32)
+        for feeder in feeders(place, p):
+            sum_copy(feeder, p).wait_recv()
+            value = value + arrived[PLACES.index(feeder), here].astype(F32)
         return value.astype(BF16)
 
-    below = at_z(-1)
     for p in range(PIECES):
-        for slot, place in enumerate(PLACES):
-            if relay_of(place) and goes(place, p):
-                own_sum_copy(slot, p).start()
-    for p in range(PIECES):
-        for slot, place in enumerate(PLACES):
-            if not relay_of(place):
-                own_sum_copy(slot, p).start()
+        for place in PLACES:
+            if goes(place, p) and not feeders(place, p):
+                sum_copy(place, p).start()
     loads[2].wait()
     loads[3].wait()
-    lax.fori_loop(0, half_rows // 144, lambda i, c: (factor_block(i), c)[1], 0)
-    for p in range(PIECES):
-        for index, relay in enumerate(RELAYS):
-            slots = [
-                slot
-                for slot, place in enumerate(PLACES)
-                if relay_of(place) == relay and goes(place, p)
-            ]
-            relayed[index, pl.ds(p * piece, piece)] = added(wrapped(d - relay, n_dp), slots, p)
-            relay_sum_copy(index, p).start()
-    lax.fori_loop(0, HIDDEN_EARLY, lambda i, c: (hidden_block(i), c)[1], 0)
-
-    def gather_copy(kind, chunk, p, target):
-        tiles = tiles_of(chunk, p)
+    links = [c for c in CHAIN if 0 < c < n_dp // 2]
+    factor_steps = half_rows // 144
+    for number, link in enumerate(links):
+        if number < factor_steps:
+            factor_block(number)
+        for p in range(PIECES):
+            for place in (link, -link):
+                relayed[PLACES.index(place), pl.ds(p * piece, piece)] = added(place, p)
+                sum_copy(place, p).start()
+    for number in range(len(links), factor_steps):
+        factor_block(number)
+
+    def gather_copy(place, p):
+        tiles = tiles_of(wrapped(d - inward(place), n_dp), p)
+        slot = PLACES.index(place)
         return pltpu.make_async_remote_copy(
             src_ref=delta.at[tiles],
             dst_ref=delta.at[tiles],
-            send_sem=gather_sems.at[0, kind, p],
-            recv_sem=gather_sems.at[1, kind, p],
-            device_id=target,
+            send_sem=gather_sems.at[0, slot, p],
+            recv_sem=gather_sems.at[1, slot, p],
+            device_id=at_z(place - inward(place)),
             device_id_type=MESH,
         )
 
-    def source_copy(kind, p):
-        step = RELAYS[kind - len(PLACES)] if kind >= len(PLACES) else PLACES[kind]
-        return gather_copy(kind, d, p, at_z(step))
-
-    def relay_copy(kind, p):
-        place = PLACES[kind]
-        relay = relay_of(place)
-        return gather_copy(kind, wrapped(d - relay, n_dp), p, at_z(place - relay))
-
-    near = [slot for slot, place in enumerate(PLACES) if not relay_of(place)]
-    far = [len(PLACES) + index for index in range(len(RELAYS))]
     for p in range(PIECES):
-        delta[tiles_of(d, p)] = added(d, near + far, p)
-        for kind in far:
-            source_copy(kind, p).start()
-    for p in range(PIECES):
-        for kind in near:
-            source_copy(kind, p).start()
+        delta[tiles_of(d, p)] = added(0, p)
+        for place in feeders(0, p):
+            gather_copy(place, p).start()
     loads[4].wait()
     loads[8].wait()
-    lax.fori_loop(0, rows // 128, lambda i, c: (norm_block(i), c)[1], 0)
-    for p in range(PIECES):
-        for index, relay in enumerate(RELAYS):
-            source_copy(far[index], p).wait_recv()
-            for kind, place in enumerate(PLACES):
-                if relay_of(place) == relay and goes(place, p):
-                    relay_copy(kind, p).start()
-    lax.fori_loop(HIDDEN_EARLY, rows // 144, lambda i, c: (hidden_block(i), c)[1], 0)
+    norm_block(0)
+    hidden_steps = rows // 144
+    norm_steps = rows // 128
+    links = links[::-1]
+    ends = [i * hidden_steps // len(links) for i in range(len(links) + 1)]
+    norm_ends = [1 + i * (norm_steps - 1) // len(links) for i in range(len(links) + 1)]
+    for number, link in enumerate(links):
+        for p in range(PIECES):
+            for place in (link, -link):
+                gather_copy(place, p).wait_recv()
+                for fed in feeders(place, p):
+                    gather_copy(fed, p).start()
+        lax.fori_loop(ends[number], ends[number + 1], lambda i, c: (hidden_block(i), c)[1], 0)
+        lax.fori_loop(
+            norm_ends[number], norm_ends[number + 1], lambda i, c: (norm_block(i), c)[1], 0
+        )
     down_grad[...] = down_total[...].astype(BF16)
     loads[5].wait()
     loads[6].wait()
     loads[7].wait()
     for p in range(PIECES):
-        for kind, place in enumerate(PLACES):
-            if goes(place, p):
-                gather_copy(kind, d, p, below).wait_recv()
+        for place in PLACES:
+            if goes(place, p) and abs(place) not in links:
+                gather_copy(place, p).wait_recv()
 
     def gate_block(i, carry):
         block = row_block(i * 16, 16)
@@ -591,10 +577,10 @@
         target[...] = (weight_own[index] + weight_in[index].astype(F32)).astype(BF16)
 
     for p in range(PIECES):
-        for kind in range(len(PLACES) + len(RELAYS)):
-            if kind in far or goes(PLACES[kind], p):
-                sum_copy(kind, p, partial.at[tiles_of(d, p)], below).wait_send()
-                gather_copy(kind, d, p, below).wait_send()
+        for place in PLACES:
+            if goes(place, p):
+                sum_copy(place, p).wait_send()
+                gather_copy(place, p).wait_send()
 
     def drain_z(i, carry):
         z_copy(i, wrapped(d + i, n_dp), d).wait_send()
@@ -630,14 +616,8 @@
 
 def hand_on(*refs):
     count = len(refs) // 2
-    sems = refs[-1]
-    copies = [
-        pltpu.make_async_copy(refs[i], refs[count + i], sems.at[i]) for i in range(count)
-    ]
-    for copy in copies:
-        copy.start()
-    for copy in copies:
-        copy.wait()
+    for source, target in zip(refs[:count], refs[count:]):
+        target[...] = source[...]
 
 
 def shards(
@@ -664,7 +644,7 @@
     group_rows = half_rows // groups
     tiles = half_rows // 16 * (hidden // 128)
     chunk_tiles = -(-tiles // (n_dp * PIECES)) * PIECES
-    ways = len(PLACES) + len(RELAYS)
+    ways = len(PLACES)
     padded = -(-half_rows // 128) * 128
     vmem = pl.BlockSpec(memory_space=pltpu.VMEM)
     hbm = pl.BlockSpec(memory_space=pl.ANY)
@@ -701,7 +681,7 @@
             pltpu.VMEM((rows, 128), F32),
             pltpu.VMEM((n_dp * chunk_tiles, 16, 128), BF16),
             pltpu.VMEM((ways, chunk_tiles, 16, 128), BF16),
-            pltpu.VMEM((len(RELAYS), chunk_tiles, 16, 128), BF16),
+            pltpu.VMEM((ways, chunk_tiles, 16, 128), BF16),
             pltpu.VMEM((n_dp * chunk_tiles, 16, 128), BF16),
             pltpu.VMEM((half_rows, hidden), F32),
             pltpu.VMEM((half_rows, hidden), F32),
@@ -752,9 +732,8 @@
     return pl.pallas_call(
         hand_on,
         out_shape=out_shape,
-        in_specs=[hbm] * 5,
-        out_specs=(hbm,) * 5,
-        scratch_shapes=[dma((5,))],
+        in_specs=[vmem] * 5,
+        out_specs=(vmem,) * 5,
     )(*grads)
 
 

time: 114 us -> 81.4 us (0.71)
  Pallas kernels: 113 us -> 80.1 us
    pallas_call x1, Pallas kernels: 25.1 us -> 2.1 us  [shards(): pl.pallas_call(hand_on, out_shape=out_shape, in_specs=[vmem] * 5, out_spe...]
    pallas_call x1, Pallas kernels: 87.7 us -> 78 us  [shards(): pl.pallas_call(functools.partial(kernel, size), out_shape=out_shape, in_s...]
where the time goes in v3:
time: 81.4 us; the launch traced here: 80.7 us
  Pallas kernels  80.1 us (98%)
    pallas_call x1, Pallas kernels, shards(): pl.pallas_call(functools.partial(kernel, size), out_shape=out_shape, in_s...  78 us
    pallas_call x1, Pallas kernels, shards(): pl.pallas_call(hand_on, out_shape=out_shape, in_specs=[vmem] * 5, out_spe...  2.1 us

profile of v3, /device:TPU:6, one launch (start us, length us, event | category | flops | bytes accessed | tf_op | source)
XLA Modules:
  0.0 80.7 jit_solution(1445461509065697945)
XLA Ops:
  0.6 78.0 %shard_map.164 = (bf16[72,256]{1,0:T(8,128)(2,1)}, bf16[256,128]{1,0:T(8,128)(2,1)}, bf16[128,896]{1,0:T(8,128)(2,1)}, bf16[128,896]{1,0:T(8,128)(2,1)}, bf16[896,128]{1,0:T(8,128)(2,1)}) custom-call(bf16[1152,256]{1,0:T(8,128)(2,1)} %context_hbm.1, bf16[1152,256]{1,0:T(8,128)(2,1)} %residual_hbm.1, f32[1152]{0:T(1024)} %rms_hbm.1, f32[1,256]{1,0:T(1,128)} %bitcast.4, ...), custom_call_target="tpu_custom_call" | custom-call | tf_op jit(solution)/shard_map/pallas_call | solution.py:664
  78.6 2.1 %shard_map.165 = (bf16[72,256]{1,0:T(8,128)(2,1)}, bf16[256,128]{1,0:T(8,128)(2,1)}, bf16[128,896]{1,0:T(8,128)(2,1)}, bf16[128,896]{1,0:T(8,128)(2,1)}, bf16[896,128]{1,0:T(8,128)(2,1)}) custom-call(bf16[72,256]{1,0:T(8,128)(2,1)} %get-tuple-element.10.refs_0_, bf16[256,128]{1,0:T(8,128)(2,1)} %get-tuple-element.11.refs_1_, ...), custom_call_target="tpu_custom_call" | custom-call | tf_op jit(solution)/shard_map/pallas_call | solution.py:732

commit v4 on v3

--- a/solution.py
+++ b/solution.py
@@ -83,6 +83,7 @@
     delta,
     gate_factor,
     up_factor,
+    dot_factor,
     gate_delta,
     up_delta,
     down_total,
@@ -94,6 +95,8 @@
     dot_z,
     dot_plane,
     dot_column,
+    base,
+    pull,
     grads,
     grad_groups,
     weight_out,
@@ -209,8 +212,14 @@
         gate_value = gate[source, :].astype(F32)
         up_value = up[source, :].astype(F32)
         squash = jax.nn.sigmoid(gate_value)
-        gate_factor[block, :] = up_value * squash * (1.0 + gate_value * (1.0 - squash))
-        up_factor[block, :] = gate_value * squash
+        gate_part = up_value * squash * (1.0 + gate_value * (1.0 - squash))
+        up_part = gate_value * squash
+        gate_factor[block, :] = gate_part
+        up_factor[block, :] = up_part
+        gained = (residual[source, :].astype(F32) * gain_row[...]).astype(BF16)
+        dot_factor[block, :] = gate_part * jnp.dot(
+            gained, gate_weight[...], preferred_element_type=F32
+        ) + up_part * jnp.dot(gained, up_weight[...], preferred_element_type=F32)
 
     def hidden_block(i):
         block = row_block(i * 144, 144)
@@ -263,13 +272,19 @@
             value = value + arrived[PLACES.index(feeder), here].astype(F32)
         return value.astype(BF16)
 
-    for p in range(PIECES):
-        for place in PLACES:
-            if goes(place, p) and not feeders(place, p):
-                sum_copy(place, p).start()
-    loads[2].wait()
-    loads[3].wait()
     links = [c for c in CHAIN if 0 < c < n_dp // 2]
+
+    def join(number):
+        link = (links + [0])[number] if number <= len(links) else None
+        for p in range(PIECES):
+            for place in PLACES:
+                if abs(inward(place)) == link and goes(place, p) and not feeders(place, p):
+                    sum_copy(place, p).start()
+
+    join(0)
+    join(1)
+    for load in loads[2:7]:
+        load.wait()
     factor_steps = half_rows // 144
     for number, link in enumerate(links):
         if number < factor_steps:
@@ -278,6 +293,7 @@
             for place in (link, -link):
                 relayed[PLACES.index(place), pl.ds(p * piece, piece)] = added(place, p)
                 sum_copy(place, p).start()
+        join(number + 2)
     for number in range(len(links), factor_steps):
         factor_block(number)
 
@@ -293,11 +309,77 @@
             device_id_type=MESH,
         )
 
+    def gate_block(i, carry):
+        block = row_block(i * 16, 16)
+        value = jnp.concatenate(
+            [delta[i * lane_tiles + c] for c in range(lane_tiles)], axis=1
+        ).astype(F32)
+        gate_delta[block, :] = (value * gate_factor[block, :]).astype(BF16)
+        up_delta[block, :] = (value * up_factor[block, :]).astype(BF16)
+        dots = value * dot_factor[block, :]
+        row_products[block, :] = sum(
+            dots[:, 128 * c : 128 * c + 128] for c in range(lane_tiles)
+        )
+        return carry
+
+
+    def share_copy(slot, owner, source):
+        return pltpu.make_async_remote_copy(
+            src_ref=share_out.at[slot],
+            dst_ref=share_in.at[source],
+            send_sem=share_sems.at[0, slot],
+            recv_sem=share_sems.at[1, source],
+            device_id=(d, s, owner),
+            device_id_type=MESH,
+        )
+
+    def share_block(i, carry):
+        block = row_block(i * pair_rows, pair_rows)
+        product = dot_nt(gate_delta[block, :], gate_weight[...]) + dot_nt(
+            up_delta[block, :], up_weight[...]
+        )
+        for q in range(2):
+            for c in range(2):
+                owner = 4 * i + 2 * q + c
+                share_out[owner] = product[
+                    q * group_rows : (q + 1) * group_rows, 128 * c : 128 * c + 128
+                ].astype(BF16)
+
+                @pl.when(owner != t)
+                def _():
+                    share_copy(owner, owner, t).start()
+
+                @pl.when(owner == t)
+                def _():
+                    share_in[t] = share_out[t]
+
+        return carry
+
+    pair_tiles = pair_rows // 16
+
+    def token_block(i):
+        lax.fori_loop(i * pair_tiles, (i + 1) * pair_tiles, gate_block, 0)
+        share_block(i, 0)
+
+    row_products[half_rows:, :] = jnp.zeros((row_products.shape[0] - half_rows, 128), F32)
+    here = d // (n_dp // half_pairs)
+    lean = lax.rem(d, n_dp // half_pairs)
+    early = lean < n_dp // half_pairs // 2
+    beside = jnp.where(early, here + half_pairs - 1, here + 1)
+    across = jnp.where(early, here + 1, here + half_pairs - 1)
+    arrived_places = set()
+
+    def reach(limit):
+        for p in range(PIECES):
+            for place in PLACES:
+                if abs(place) <= limit and goes(place, p) and (place, p) not in arrived_places:
+                    arrived_places.add((place, p))
+                    gather_copy(place, p).wait_recv()
+
     for p in range(PIECES):
         delta[tiles_of(d, p)] = added(0, p)
         for place in feeders(0, p):
             gather_copy(place, p).start()
-    loads[4].wait()
     loads[8].wait()
     norm_block(0)
     hidden_steps = rows // 144
@@ -308,6 +390,7 @@
     for number, link in enumerate(links):
         for p in range(PIECES):
             for place in (link, -link):
+                arrived_places.add((place, p))
                 gather_copy(place, p).wait_recv()
                 for fed in feeders(place, p):
                     gather_copy(fed, p).start()
@@ -315,63 +398,17 @@
         lax.fori_loop(
             norm_ends[number], norm_ends[number + 1], lambda i, c: (norm_block(i), c)[1], 0
         )
+        if link == 4:
+            reach(4)
+            token_block(here)
+        if link == 6:
+            reach(6)
+            token_block(lax.rem(beside, half_pairs))
     down_grad[...] = down_total[...].astype(BF16)
-    loads[5].wait()
-    loads[6].wait()
     loads[7].wait()
-    for p in range(PIECES):
-        for place in PLACES:
-            if goes(place, p) and abs(place) not in links:
-                gather_copy(place, p).wait_recv()
-
-    def gate_block(i, carry):
-        block = row_block(i * 16, 16)
-        value = jnp.concatenate(
-            [delta[i * lane_tiles + c] for c in range(lane_tiles)], axis=1
-        ).astype(F32)
-        gate_delta[block, :] = (value * gate_factor[block, :]).astype(BF16)
-        up_delta[block, :] = (value * up_factor[block, :]).astype(BF16)
-        return carry
-
-    lax.fori_loop(0, half_rows // 16, gate_block, 0)
-
-    def share_copy(slot, owner, source):
-        return pltpu.make_async_remote_copy(
-            src_ref=share_out.at[slot],
-            dst_ref=share_in.at[source],
-            send_sem=share_sems.at[0, slot],
-            recv_sem=share_sems.at[1, source],
-            device_id=(d, s, owner),
-            device_id_type=MESH,
-        )
-
-    def share_block(i, carry):
-        block = row_block(i * pair_rows, pair_rows)
-        source = row_block(row_base + i * pair_rows, pair_rows)
-        product = dot_nt(gate_delta[block, :], gate_weight[...]) + dot_nt(
-            up_delta[block, :], up_weight[...]
-        )
-        for q in range(2):
-            for c in range(2):
-                owner = 4 * i + 2 * q + c
-                share_out[owner] = product[
-                    q * group_rows : (q + 1) * group_rows, 128 * c : 128 * c + 128
-                ].astype(BF16)
-
-                @pl.when(owner != t)
-                def _():
-                    share_copy(owner, owner, t).start()
-
-                @pl.when(owner == t)
-                def _():
-                    share_in[t] = share_out[t]
-
-        scaled = product * residual[source, :].astype(F32) * gain_row[...]
-        row_products[block, :] = scaled[:, :128] + scaled[:, 128:]
-        return carry
-
-    row_products[half_rows:, :] = jnp.zeros((row_products.shape[0] - half_rows, 128), F32)
-    lax.fori_loop(0, half_pairs, share_block, 0)
+    reach(n_dp // 2)
+    token_block(lax.rem(here + 2, half_pairs))
+    token_block(lax.rem(across, half_pairs))
 
     def z_copy(slot, peer, source):
         return pltpu.make_async_remote_copy(
@@ -497,6 +534,39 @@
     weight_own[0] = dot_tn(normed[own_normed_rows, own_cols], gate_delta[...])
     weight_own[1] = dot_tn(normed[own_normed_rows, own_cols], up_delta[...])
 
+    def wait_spread(group, carry):
+        side = group // groups
+        owner = 2 * lax.rem(group, groups) + s
+
+        @pl.when(jnp.logical_not((side == s) & (owner == t)))
+        def _():
+            spread_copy(0, t, group).wait_recv()
+
+        return carry
+
+    lax.fori_loop(0, n_tensor, wait_spread, 0)
+
+    scale = 1.0 / (features * n_dp)
+
+    def finish(weighted_value, residual_value, rms_value, gain_value, delta_value, dot_value):
+        row_scale = rms_value * rms_value * rms_value * dot_value * scale
+        return weighted_value + rms_value * gain_value * delta_value - residual_value * row_scale
+
+    def base_block(i, carry):
+        block = row_block(i * pair_rows, pair_rows)
+        rms_value = rms[block, :]
+        base[block, :] = weighted[block, own_cols].astype(F32) + rms_value * gain_row[
+            :, own_cols
+        ] * jnp.concatenate(
+            [normed_delta[2 * i].astype(F32), normed_delta[2 * i + 1].astype(F32)], axis=0
+        )
+        pull[block, :] = residual[block, own_cols].astype(F32) * (
+            rms_value * rms_value * rms_value * scale
+        )
+        return carry
+
+    lax.fori_loop(0, n_tensor // 2, base_block, 0)
+
     def wait_plane(i, carry):
         plane_copy(i, wrapped(me + i, n_plane)).wait_recv()
         return carry
@@ -510,38 +580,11 @@
             cols = slice(128 * b, 128 * b + 128)
             dot_column[side, cols, :] = jnp.transpose(jnp.broadcast_to(line[:, cols], (128, 128)))
 
-    def wait_spread(group, carry):
-        side = group // groups
-        owner = 2 * lax.rem(group, groups) + s
-
-        @pl.when(jnp.logical_not((side == s) & (owner == t)))
-        def _():
-            spread_copy(0, t, group).wait_recv()
-
-        return carry
-
-    lax.fori_loop(0, n_tensor, wait_spread, 0)
-
-    scale = 1.0 / (features * n_dp)
-
-    def finish(weighted_value, residual_value, rms_value, gain_value, delta_value, dot_value):
-        row_scale = rms_value * rms_value * rms_value * dot_value * scale
-        return weighted_value + rms_value * gain_value * delta_value - residual_value * row_scale
-
     def finish_block(i, carry):
         block = row_block(i * pair_rows, pair_rows)
         side = i // half_pairs
         local = row_block((i - side * half_pairs) * pair_rows, pair_rows)
-        value = finish(
-            weighted[block, own_cols].astype(F32),
-            residual[block, own_cols].astype(F32),
-            rms[block, :],
-            gain_row[:, own_cols],
-            jnp.concatenate(
-                [normed_delta[2 * i].astype(F32), normed_delta[2 * i + 1].astype(F32)], axis=0
-            ),
-            dot_column[side, local, :],
-        )
+        value = base[block, :] - pull[block, :] * dot_column[side, local, :]
         grads[block, :] = value.astype(BF16)
         grad_groups[2 * i] = value[:group_rows].astype(BF16)
         grad_groups[2 * i + 1] = value[group_rows:].astype(BF16)
@@ -685,6 +728,7 @@
             pltpu.VMEM((n_dp * chunk_tiles, 16, 128), BF16),
             pltpu.VMEM((half_rows, hidden), F32),
             pltpu.VMEM((half_rows, hidden), F32),
+            pltpu.VMEM((half_rows, hidden), F32),
             pltpu.VMEM((half_rows, hidden), BF16),
             pltpu.VMEM((half_rows, hidden), BF16),
             pltpu.VMEM((hidden, features // 2), F32),
@@ -696,6 +740,8 @@
             pltpu.VMEM((n_dp, 1, padded), F32),
             pltpu.VMEM((2 * n_tensor, 1, padded), F32),
             pltpu.VMEM((2, padded, 128), F32),
+            pltpu.VMEM((rows, 128), F32),
+            pltpu.VMEM((rows, 128), F32),
             pltpu.VMEM((rows, 128), BF16),
             pltpu.VMEM((n_tensor, group_rows, 128), BF16),
             pltpu.VMEM((2, features // 2, hidden), BF16),

time: 81.4 us -> 78.8 us (0.968)
  Pallas kernels: 80.1 us -> 78 us
    pallas_call x1, Pallas kernels: 78 us -> 75.9 us  [shards(): pl.pallas_call(functools.partial(kernel, size), out_shape=out_shape, in_s...]
where the time goes in v4:
time: 78.8 us; the launch traced here: 78.6 us
  Pallas kernels  78 us (99%)
    pallas_call x1, Pallas kernels, shards(): pl.pallas_call(functools.partial(kernel, size), out_shape=out_shape, in_s...  75.9 us
    pallas_call x1, Pallas kernels, shards(): pl.pallas_call(hand_on, out_shape=out_shape, in_specs=[vmem] * 5, out_spe...  2.1 us

profile of v4, /device:TPU:6, one launch (start us, length us, event | category | flops | bytes accessed | tf_op | source)
XLA Modules:
  0.0 78.6 jit_solution(2691552071661634300)
XLA Ops:
  0.6 75.9 %shard_map.164 = (bf16[72,256]{1,0:T(8,128)(2,1)}, bf16[256,128]{1,0:T(8,128)(2,1)}, bf16[128,896]{1,0:T(8,128)(2,1)}, bf16[128,896]{1,0:T(8,128)(2,1)}, bf16[896,128]{1,0:T(8,128)(2,1)}) custom-call(bf16[1152,256]{1,0:T(8,128)(2,1)} %context_hbm.1, bf16[1152,256]{1,0:T(8,128)(2,1)} %residual_hbm.1, f32[1152]{0:T(1024)} %rms_hbm.1, f32[1,256]{1,0:T(1,128)} %bitcast.4, ...), custom_call_target="tpu_custom_call" | custom-call | tf_op jit(solution)/shard_map/pallas_call | solution.py:707
  76.5 2.1 %shard_map.165 = (bf16[72,256]{1,0:T(8,128)(2,1)}, bf16[256,128]{1,0:T(8,128)(2,1)}, bf16[128,896]{1,0:T(8,128)(2,1)}, bf16[128,896]{1,0:T(8,128)(2,1)}, bf16[896,128]{1,0:T(8,128)(2,1)}) custom-call(bf16[72,256]{1,0:T(8,128)(2,1)} %get-tuple-element.10.refs_0_, bf16[256,128]{1,0:T(8,128)(2,1)} %get-tuple-element.11.refs_1_, ...), custom_call_target="tpu_custom_call" | custom-call | tf_op jit(solution)/shard_map/pallas_call | solution.py:778

commit v5 on v4

--- a/solution.py
+++ b/solution.py
@@ -10,7 +10,7 @@
 
 POS = 36
 LEN = 4096
-PIECES = 4
+PIECES = 2
 PLACES = (8, -8, 7, -7, 6, -6, 5, -5, 4, -4, 3, -3, 2, -2, 1, -1)
 CHAIN = (8, 6, 4, 2, 0)
 MESH = pl.DeviceIdType.MESH

time: 78.8 us -> 77.6 us (0.985)
  Pallas kernels: 78 us -> 76.3 us
    pallas_call x1, Pallas kernels: 75.9 us -> 74.2 us  [shards(): pl.pallas_call(functools.partial(kernel, size), out_shape=out_shape, in_s...]
where the time goes in v5:
time: 77.6 us; the launch traced here: 77 us
  Pallas kernels  76.3 us (98%)
    pallas_call x1, Pallas kernels, shards(): pl.pallas_call(functools.partial(kernel, size), out_shape=out_shape, in_s...  74.2 us
    pallas_call x1, Pallas kernels, shards(): pl.pallas_call(hand_on, out_shape=out_shape, in_specs=[vmem] * 5, out_spe...  2.1 us

profile of v5, /device:TPU:6, one launch (start us, length us, event | category | flops | bytes accessed | tf_op | source)
XLA Modules:
  0.0 77.0 jit_solution(13744331131098184599)
XLA Ops:
  0.6 74.2 %shard_map.164 = (bf16[72,256]{1,0:T(8,128)(2,1)}, bf16[256,128]{1,0:T(8,128)(2,1)}, bf16[128,896]{1,0:T(8,128)(2,1)}, bf16[128,896]{1,0:T(8,128)(2,1)}, bf16[896,128]{1,0:T(8,128)(2,1)}) custom-call(bf16[1152,256]{1,0:T(8,128)(2,1)} %context_hbm.1, bf16[1152,256]{1,0:T(8,128)(2,1)} %residual_hbm.1, f32[1152]{0:T(1024)} %rms_hbm.1, f32[1,256]{1,0:T(1,128)} %bitcast.4, ...), custom_call_target="tpu_custom_call" | custom-call | tf_op jit(solution)/shard_map/pallas_call | solution.py:707
  74.9 2.1 %shard_map.165 = (bf16[72,256]{1,0:T(8,128)(2,1)}, bf16[256,128]{1,0:T(8,128)(2,1)}, bf16[128,896]{1,0:T(8,128)(2,1)}, bf16[128,896]{1,0:T(8,128)(2,1)}, bf16[896,128]{1,0:T(8,128)(2,1)}) custom-call(bf16[72,256]{1,0:T(8,128)(2,1)} %get-tuple-element.10.refs_0_, bf16[256,128]{1,0:T(8,128)(2,1)} %get-tuple-element.11.refs_1_, ...), custom_call_target="tpu_custom_call" | custom-call | tf_op jit(solution)/shard_map/pallas_call | solution.py:778
